TPU v7x, 512 devices: a whole 4x8x8 slice. The times are simulated.
512 devices in a mesh: rep: 16 (over x_lo, z), fsdp: 32 (over y, x_hi, core).
Axes of the slice: x: 4 (x_hi: 2, x_lo: 2; x = x_hi * 2 + x_lo), y: 8, z: 8, core: 2. Of those that a mesh axis runs over, the one named last changes fastest.
Arguments:
- hidden: bfloat16 [65536, 8192], P(('rep', 'fsdp')), may hold values from -24 to 24
- gain: float32 [8192], replicated, may hold values from 0.1 to 1.9
- key_weight: bfloat16 [16, 8192, 512], P('rep', 'fsdp'), may hold values from -6 to 6
- moment: float32 [16, 8192, 512], P('rep', 'fsdp'), may hold values from -4 to 4
- second: float32 [16, 8192, 512], P('rep', 'fsdp'), may hold values from 0.05 to 1
- dkeys: bfloat16 [65536, 512], P(('rep', 'fsdp')), may hold values from -6 to 6
- step: int32 [], replicated, may hold values from 0 to 29
Outputs:
- keys: bfloat16 [65536, 512], P(('rep', 'fsdp'))
- new_weight: bfloat16 [16, 8192, 512], P('rep', 'fsdp')
- new_moment: float32 [16, 8192, 512], P('rep', 'fsdp')
- new_second: float32 [16, 8192, 512], P('rep', 'fsdp')
All inputs are finite; a program needn't handle non-finite values.
Results may differ from a plain program's by a relative error of at most 0.0051.
Values may be sent and summed in bfloat16 or wider, within the bound.
No kernel may reach another device: no remote copies, remote signals or barrier semaphores. Data moves between devices by JAX's collectives and lax.ppermute only.
A program may use at most 64 MiB of HBM per device.

v0:
```python
import functools
import math

import jax
import jax.numpy as jnp
from jax import lax
from jax.experimental import pallas as pl
from jax.experimental.pallas import tpu as pltpu
from jax.sharding import Mesh
from jax.sharding import PartitionSpec as P


HEAD = 128
NY, NP = 8, 4
GROUP = ("y", "x", "c")
PLANE = ("x", "c")
EVERY = ("rep", "y", "x", "c")
DISTANCES = (1, 2, 4)
SENDS = (1, 2, 3, 4, 7, 6, 5)
BF16, F32 = jnp.bfloat16, jnp.float32


def shifted(block, distance):
    return lax.ppermute(block, "y", [(i, (i + distance) % NY) for i in range(NY)])


def across(block, axis):
    return lax.ppermute(block, axis, [(0, 1), (1, 0)])


def vmem(count):
    return [pl.BlockSpec(memory_space=pltpu.VMEM)] * count


SMEM = pl.BlockSpec(memory_space=pltpu.SMEM)


def cost(flops, nbytes):
    return pl.CostEstimate(flops=flops, bytes_accessed=nbytes, transcendentals=0)


def turn(values, cosine, sine):
    return values * cosine + pltpu.roll(values, HEAD // 2, 1) * sine


def norm_kernel(y_ref, rows_ref, gain_ref, out_ref):
    values = rows_ref[...].astype(F32)
    inverse = lax.rsqrt(jnp.mean(values * values, axis=-1, keepdims=True) + 1e-05)
    feat = rows_ref.shape[1] // (NY * NP)
    for k in range(NY):
        block = lax.rem(y_ref[0] + k, NY)
        for p in range(NP):
            start = pl.multiple_of((block * NP + p) * feat, 128)
            part = rows_ref[:, pl.ds(start, feat)].astype(F32)
            normed = part * inverse * gain_ref[:, pl.ds(start, feat)]
            out_ref[p, :, k * feat : (k + 1) * feat] = normed.astype(BF16)


def norm(y, hidden, gain):
    rows, width = hidden.shape
    step = 32
    return pl.pallas_call(
        norm_kernel,
        grid=(rows // step,),
        in_specs=[SMEM, pl.BlockSpec((step, width), lambda i: (i, 0)), pl.BlockSpec((1, width), lambda i: (0, 0))],
        out_specs=pl.BlockSpec((NP, step, width // NP), lambda i: (0, i, 0)),
        out_shape=jax.ShapeDtypeStruct((NP, rows, width // NP), BF16),
        cost_estimate=cost(6 * rows * width, 4 * rows * width),
        name="norm",
    )(y, hidden, gain)


def turn_back_kernel(values_ref, cosine_ref, sine_ref, out_ref):
    for h in range(values_ref.shape[1] // HEAD):
        cols = slice(h * HEAD, (h + 1) * HEAD)
        turned = turn(values_ref[:, cols].astype(F32), cosine_ref[...], -sine_ref[...])
        out_ref[cols, :] = turned.T.astype(BF16)


def turn_back(values, cosine, sine):
    return pl.pallas_call(
        turn_back_kernel,
        in_specs=vmem(3),
        out_specs=pl.BlockSpec(memory_space=pltpu.VMEM),
        out_shape=jax.ShapeDtypeStruct(values.shape[::-1], BF16),
        cost_estimate=cost(4 * values.size, 4 * values.size),
        name="turn_back",
    )(values, cosine, sine)


def grads_kernel(at_ref, tokens_ref, d00, d10, d01, d11, *refs):
    outs, dpre_ref = refs[:-1], refs[-1]
    rows = d00.shape[1]
    for i, piece in enumerate((d00, d10, d01, d11)):
        dpre_ref[:, pl.ds(pl.multiple_of(at_ref[i] * rows, 128), rows)] = piece[...]
    feat = outs[0].shape[1]
    for k, out in enumerate(outs):
        block = tokens_ref[:, k * feat : (k + 1) * feat]
        out[...] = jnp.dot(dpre_ref[...], block, preferred_element_type=F32).astype(out.dtype)


def grads(at, tokens, pieces):
    count, width = tokens.shape
    kvw = pieces[0].shape[0]
    feat = width // NY
    return pl.pallas_call(
        grads_kernel,
        in_specs=[SMEM] + vmem(1 + len(pieces)),
        out_specs=vmem(NY),
        out_shape=[jax.ShapeDtypeStruct((kvw, feat), BF16 if k else F32) for k in range(NY)],
        scratch_shapes=[pltpu.VMEM((kvw, count), BF16)],
        cost_estimate=cost(2 * count * width * kvw, 2 * count * width + 3 * width * kvw),
        name="grads",
    )(at, tokens, *pieces)


def forward_kernel(tokens_ref, *refs):
    weights, out_ref = refs[:-1], refs[-1]
    feat = weights[0].shape[0]
    rows = out_ref.shape[1]
    for p in range(NP):
        mine = slice(p * rows, (p + 1) * rows)
        total = jnp.zeros(out_ref.shape[1:], F32)
        for k, weight in enumerate(weights):
            total += jnp.dot(tokens_ref[mine, k * feat : (k + 1) * feat], weight[...], preferred_element_type=F32)
        out_ref[p] = total.astype(out_ref.dtype)


def forward(tokens, weights):
    count, width = tokens.shape
    kvw = weights[0].shape[1]
    return pl.pallas_call(
        forward_kernel,
        in_specs=vmem(1 + len(weights)),
        out_specs=pl.BlockSpec(memory_space=pltpu.VMEM),
        out_shape=jax.ShapeDtypeStruct((NP, count // NP, kvw), BF16),
        cost_estimate=cost(2 * count * width * kvw, 5 << 20),
        name="forward",
    )(tokens, *weights)


def keys_kernel(scale, parts_ref, cosine_ref, sine_ref, out_ref):
    for h in range(out_ref.shape[1] // HEAD):
        cols = slice(h * HEAD, (h + 1) * HEAD)
        total = parts_ref[0, :, cols].astype(F32)
        for p in range(1, NP):
            total = total + parts_ref[p, :, cols].astype(F32)
        out_ref[:, cols] = turn(total * scale, cosine_ref[...], sine_ref[...]).astype(BF16)


def finish_keys(parts, cosine, sine, scale):
    return pl.pallas_call(
        functools.partial(keys_kernel, scale),
        in_specs=vmem(3),
        out_specs=pl.BlockSpec(memory_space=pltpu.VMEM),
        out_shape=jax.ShapeDtypeStruct(parts.shape[1:], BF16),
        cost_estimate=cost(8 * parts.size, 2 * parts.size),
        name="finish_keys",
    )(parts, cosine, sine)


def update_kernel(scale, bias_ref, moment_ref, second_ref, weight_ref, *refs):
    arrived, (moment_out, second_out, local_out) = refs[:-3], refs[-3:]
    total = arrived[0][...]
    for part in arrived[1:]:
        total = total + part[...].astype(F32)
    grad = total.T * scale
    moment = 0.9 * moment_ref[...] + 0.1 * grad
    second = 0.95 * second_ref[...] + 0.05 * grad * grad
    moment_out[...] = moment
    second_out[...] = second
    mhat = moment / bias_ref[0]
    vhat = second / bias_ref[1]
    weight = weight_ref[...].astype(F32)
    local_out[...] = (weight - 0.05 * (mhat / (jnp.sqrt(vhat) + 1e-08) + 0.1 * weight)).astype(BF16)


def update(bias, moment, second, weight, arrived, scale):
    feat, kvw = weight.shape
    step = 128
    flat = pl.BlockSpec((step, kvw), lambda i: (i, 0))
    turned = pl.BlockSpec((kvw, step), lambda i: (0, i))
    return pl.pallas_call(
        functools.partial(update_kernel, scale),
        grid=(feat // step,),
        in_specs=[SMEM] + [flat] * 3 + [turned] * len(arrived),
        out_specs=[flat] * 3,
        out_shape=[jax.ShapeDtypeStruct((feat, kvw), kind) for kind in (F32, F32, BF16)],
        cost_estimate=cost(30 * feat * kvw, 34 * feat * kvw),
        name="update",
    )(bias, moment, second, weight, *arrived)


def rotation(positions):
    half = HEAD // 2
    freq = jnp.exp(jnp.arange(half).astype(F32) * (-2.0 * math.log(500000.0) / HEAD))
    angle = positions.astype(F32)[:, None] * freq[None, :]
    cosine, sine = jnp.cos(angle), jnp.sin(angle)
    return jnp.concatenate([cosine, cosine], 1), jnp.concatenate([-sine, sine], 1)


def one_distance(number, hidden, gain, key_weight, moment, second, dkeys, step):
    rows, width = hidden.shape
    scale = width ** (-0.5)
    weight = key_weight[0]
    y, x, c = [lax.axis_index(axis).astype(jnp.int32) for axis in GROUP]

    tokens = norm(y.reshape(1), hidden, gain.reshape(1, -1))
    tokens = lax.all_to_all(tokens, PLANE, 0, 0, tiled=True).reshape(NP * rows, -1)

    positions = lax.axis_index(GROUP) * rows + jnp.arange(rows)
    cosine, sine = rotation(positions)
    own = turn_back(dkeys, cosine, sine)
    beside = across(own, "x")
    other = across(own, "c")
    corner = across(beside, "c")

    held = {0: weight}
    for k in (1, 2, 3, 4):
        held[NY - k] = shifted(held[(NY + 1 - k) % NY], 1)
        if k < 4:
            held[k] = shifted(held[k - 1], -1)

    at = jnp.stack([x * 2 + c, (1 - x) * 2 + c, x * 2 + 1 - c, (1 - x) * 2 + 1 - c])
    blocks = grads(at, tokens, (own, beside, other, corner))
    arrived = [blocks[0]]
    for k in SENDS:
        arrived.append(shifted(blocks[k], k))

    parts = forward(tokens, [held[k] for k in range(NY)])
    parts = lax.all_to_all(parts, PLANE, 0, 0, tiled=True)
    keys = finish_keys(parts, cosine, sine, scale)

    count = (step + 1).astype(F32)
    bias = jnp.stack([1.0 - jnp.power(F32(0.9), count), 1.0 - jnp.power(F32(0.95), count)])
    new_moment, new_second, local = update(bias, moment[0], second[0], weight, arrived, scale)
    groups = lax.axis_size("rep")
    distance = DISTANCES[number]
    other = lax.ppermute(local, "rep", [((i - distance) % groups, i) for i in range(groups)])
    new_weight = ((local.astype(F32) + other.astype(F32)) * 0.5).astype(BF16)
    return (keys, new_weight[None], new_moment[None], new_second[None])


def per_device(*args):
    def branch(number):
        def run(*args):
            return one_distance(number, *args)

        return run

    return lax.switch(args[-1] % len(DISTANCES), [branch(n) for n in range(len(DISTANCES))], *args)


def solution(mesh):
    finer = Mesh(mesh.devices.reshape(mesh.shape["rep"], NY, 2, 2), EVERY)
    placed = (
        P(EVERY, None),
        P(),
        P("rep", GROUP, None),
        P("rep", GROUP, None),
        P("rep", GROUP, None),
        P(EVERY, None),
        P(),
    )
    return jax.shard_map(
        per_device,
        mesh=finer,
        in_specs=placed,
        out_specs=(P(EVERY, None), P("rep", GROUP, None), P("rep", GROUP, None), P("rep", GROUP, None)),
        check_vma=False,
    )
```

profile of v0, /device:TPU:60, one launch (start us, length us, event | category | flops | bytes accessed | tf_op | source)
XLA Modules:
  0.0 147.5 jit_solution(1528001141898685908)
XLA Ops:
  1.3 146.2 %conditional.1 = (bf16[128,512]{1,0:T(8,128)(2,1)}, bf16[1,256,512]{2,1,0:T(8,128)(2,1)}, f32[1,256,512]{2,1,0:T(8,128)}, f32[1,256,512]{2,1,0:T(8,128)}) conditional(s32[]{:T(128)} %clamp.3, (f32[8192]{0:T(1024)}, bf16[128,8192]{1,0:T(8,128)(2,1)}, bf16[1,256,512]{2,1,0:T(8,128)(2,1)}, s32[]{:T(128)}, f32[1,256,512]{2,1,0:T(8,128)}, ...), branch_computations={%region_0.1_spmd, %region_1.2_spmd, %region_2.3_spmd} | conditional | flops 2160771584 | bytes 71371824 | solution.py:251
  1.3 4.3 %norm.3 = bf16[4,128,2048]{2,1,0:T(8,128)(2,1)} custom-call(s32[1]{0:T(128)} %bitcast.y_ref, bf16[128,8192]{1,0:T(8,128)(2,1)} %get-tuple-element.42.rows_ref, f32[1,8192]{1,0:T(1,128)} %bitcast.72), custom_call_target="tpu_custom_call" | custom-call | flops 6291456 | bytes 4194304 | tf_op jit(solution)/shard_map/cond/branch_0_fun/norm/pallas_call | solution.py:62
  5.7 4.9 %all-to-all-start = ((bf16[4,128,2048]{2,1,0:T(8,128)(2,1)}), bf16[4,128,2048]{2,1,0:T(8,128)(2,1)S(1)}, u32[]{:S(2)}, u32[]{:S(2)}) async-start(bf16[4,128,2048]{2,1,0:T(8,128)(2,1)} %norm.3), calls=%async_computation | async-start | bytes 4194304 | tf_op jit(solution)/shard_map/cond/branch_0_fun/all_to_all | solution.py:209
  10.6 6.3 %collective-permute-start.3 = (bf16[256,512]{1,0:T(8,128)(2,1)S(1)}, bf16[256,512]{1,0:T(8,128)(2,1)S(1)}, u32[]{:S(2)}, u32[]{:S(2)}) collective-permute-start(bf16[256,512]{1,0:T(8,128)(2,1)S(1)} %bitcast.48), channel_id=1, source_target_pairs={{0,4},{4,8},{8,12},{12,16},{16,20},{20,24},{24,28},{28,0},{1,5},{5... | collective-permute-start | bytes 786440 | tf_op jit(solution)/shard_map/cond/branch_0_fun/ppermute | solution.py:24
  16.9 1.9 %collective-permute-start = (bf16[256,512]{1,0:T(8,128)(2,1)S(1)}, bf16[256,512]{1,0:T(8,128)(2,1)S(1)}, u32[]{:S(2)}, u32[]{:S(2)}) collective-permute-start(bf16[256,512]{1,0:T(8,128)(2,1)S(1)} %bitcast.49), channel_id=1, source_target_pairs={{0,28},{4,0},{8,4},{12,8},{16,12},{20,16},{24,20},{28,24},{1,29},{... | collective-permute-start | bytes 786440 | tf_op jit(solution)/shard_map/cond/branch_0_fun/ppermute | solution.py:24
  18.9 3.9 %collective-permute-done.3.refs_7_ = bf16[256,512]{1,0:T(8,128)(2,1)S(1)} collective-permute-done((bf16[256,512]{1,0:T(8,128)(2,1)S(1)}, bf16[256,512]{1,0:T(8,128)(2,1)S(1)}, u32[]{:S(2)}, u32[]{:S(2)}) %collective-permute-start.3) | collective-permute-done | bytes 262176 | tf_op jit(solution)/shard_map/cond/branch_0_fun/ppermute | solution.py:24
  22.7 5.6 %collective-permute-start.4 = (bf16[256,512]{1,0:T(8,128)(2,1)S(1)}, bf16[256,512]{1,0:T(8,128)(2,1)S(1)}, u32[]{:S(2)}, u32[]{:S(2)}) collective-permute-start(bf16[256,512]{1,0:T(8,128)(2,1)S(1)} %collective-permute-done.3.refs_7_), channel_id=1, source_target_pairs={{0,4},{4,8},{8,12},{12,16},{16,20},{20,24},{24,28},{28,0},{1,5},{5... | collective-permute-start | bytes 786440 | tf_op jit(solution)/shard_map/cond/branch_0_fun/ppermute | solution.py:24
  29.4 1.9 %collective-permute-start.1 = (bf16[256,512]{1,0:T(8,128)(2,1)S(1)}, bf16[256,512]{1,0:T(8,128)(2,1)S(1)}, u32[]{:S(2)}, u32[]{:S(2)}) collective-permute-start(bf16[256,512]{1,0:T(8,128)(2,1)S(1)} %collective-permute-done.refs_1_), channel_id=1, source_target_pairs={{0,28},{4,0},{8,4},{12,8},{16,12},{20,16},{24,20},{28,24},{1,29},{... | collective-permute-start | bytes 786440 | tf_op jit(solution)/shard_map/cond/branch_0_fun/ppermute | solution.py:24
  31.3 2.0 %collective-permute-done.4.refs_6_ = bf16[256,512]{1,0:T(8,128)(2,1)S(1)} collective-permute-done((bf16[256,512]{1,0:T(8,128)(2,1)S(1)}, bf16[256,512]{1,0:T(8,128)(2,1)S(1)}, u32[]{:S(2)}, u32[]{:S(2)}) %collective-permute-start.4) | collective-permute-done | bytes 262176 | tf_op jit(solution)/shard_map/cond/branch_0_fun/ppermute | solution.py:24
  33.3 5.6 %collective-permute-start.5 = (bf16[256,512]{1,0:T(8,128)(2,1)S(1)}, bf16[256,512]{1,0:T(8,128)(2,1)}, u32[]{:S(2)}, u32[]{:S(2)}) collective-permute-start(bf16[256,512]{1,0:T(8,128)(2,1)S(1)} %collective-permute-done.4.refs_6_), channel_id=1, source_target_pairs={{0,4},{4,8},{8,12},{12,16},{16,20},{20,24},{24,28},{28,0},{1,5},{5... | collective-permute-start | bytes 786440 | tf_op jit(solution)/shard_map/cond/branch_0_fun/ppermute | solution.py:24
  40.7 2.6 %collective-permute-start.7 = (bf16[512,128]{1,0:T(8,128)(2,1)}, bf16[512,128]{1,0:T(8,128)(2,1)S(1)}, u32[]{:S(2)}, u32[]{:S(2)}) collective-permute-start(bf16[512,128]{1,0:T(8,128)(2,1)} %turn_back.3.d00), channel_id=1, source_target_pairs={{0,2},{2,0},{1,3},{3,1},{4,6},{6,4},{5,7},{7,5},{8,10},{10,8},{9,1... | collective-permute-start | bytes 393224 | tf_op jit(solution)/shard_map/cond/branch_0_fun/ppermute | solution.py:28
  43.3 1.9 %collective-permute-start.8 = (bf16[512,128]{1,0:T(8,128)(2,1)}, bf16[512,128]{1,0:T(8,128)(2,1)}, u32[]{:S(2)}, u32[]{:S(2)}) collective-permute-start(bf16[512,128]{1,0:T(8,128)(2,1)} %turn_back.3.d00), channel_id=1, source_target_pairs={{0,1},{1,0},{2,3},{3,2},{4,5},{5,4},{6,7},{7,6},{8,9},{9,8},{10,11... | collective-permute-start | bytes 393224 | tf_op jit(solution)/shard_map/cond/branch_0_fun/ppermute | solution.py:28
  45.2 4.0 %collective-permute-done.7.d10 = bf16[512,128]{1,0:T(8,128)(2,1)S(1)} collective-permute-done((bf16[512,128]{1,0:T(8,128)(2,1)}, bf16[512,128]{1,0:T(8,128)(2,1)S(1)}, u32[]{:S(2)}, u32[]{:S(2)}) %collective-permute-start.7) | collective-permute-done | bytes 131104 | tf_op jit(solution)/shard_map/cond/branch_0_fun/ppermute | solution.py:28
  49.3 1.9 %collective-permute-start.9 = (bf16[512,128]{1,0:T(8,128)(2,1)S(1)}, bf16[512,128]{1,0:T(8,128)(2,1)}, u32[]{:S(2)}, u32[]{:S(2)}) collective-permute-start(bf16[512,128]{1,0:T(8,128)(2,1)S(1)} %collective-permute-done.7.d10), channel_id=1, source_target_pairs={{0,1},{1,0},{2,3},{3,2},{4,5},{5,4},{6,7},{7,6},{8,9},{9,8},{10,11... | collective-permute-start | bytes 393224 | tf_op jit(solution)/shard_map/cond/branch_0_fun/ppermute | solution.py:28
  51.8 1.9 %collective-permute-start.2 = (bf16[256,512]{1,0:T(8,128)(2,1)S(1)}, bf16[256,512]{1,0:T(8,128)(2,1)}, u32[]{:S(2)}, u32[]{:S(2)}) collective-permute-start(bf16[256,512]{1,0:T(8,128)(2,1)S(1)} %collective-permute-done.1.refs_2_), channel_id=1, source_target_pairs={{0,28},{4,0},{8,4},{12,8},{16,12},{20,16},{24,20},{28,24},{1,29},{... | collective-permute-start | bytes 786440 | tf_op jit(solution)/shard_map/cond/branch_0_fun/ppermute | solution.py:24
  53.8 5.1 %collective-permute-start.6 = (bf16[256,512]{1,0:T(8,128)(2,1)}, bf16[256,512]{1,0:T(8,128)(2,1)}, u32[]{:S(2)}, u32[]{:S(2)}) collective-permute-start(bf16[256,512]{1,0:T(8,128)(2,1)} %collective-permute-done.5.refs_5_), channel_id=1, source_target_pairs={{0,4},{4,8},{8,12},{12,16},{16,20},{20,24},{24,28},{28,0},{1,5},{5... | collective-permute-start | bytes 786440 | tf_op jit(solution)/shard_map/cond/branch_0_fun/ppermute | solution.py:24
  60.2 3.9 %grads.3 = (f32[512,256]{1,0:T(8,128)}, bf16[512,256]{1,0:T(8,128)(2,1)}, bf16[512,256]{1,0:T(8,128)(2,1)}, bf16[512,256]{1,0:T(8,128)(2,1)}, bf16[512,256]{1,0:...) custom-call(s32[4]{0:T(128)} %pad_add_fusion.at_ref, ...), custom_call_target="tpu_custom_call" | custom-call | flops 1073741824 | bytes 5242880 | tf_op jit(solution)/shard_map/cond/branch_0_fun/grads/pallas_call | solution.py:106
  64.2 1.9 %collective-permute-start.10 = (bf16[512,256]{1,0:T(8,128)(2,1)}, bf16[512,256]{1,0:T(8,128)(2,1)S(1)}, u32[]{:S(2)}, u32[]{:S(2)}) collective-permute-start(bf16[512,256]{1,0:T(8,128)(2,1)} %get-tuple-element.50), channel_id=1, source_target_pairs={{0,4},{4,8},{8,12},{12,16},{16,20},{20,24},{24,28},{28,0},{1,5},{5... | collective-permute-start | bytes 786440 | tf_op jit(solution)/shard_map/cond/branch_0_fun/ppermute | solution.py:24
  66.1 1.9 %collective-permute-start.11 = (bf16[512,256]{1,0:T(8,128)(2,1)}, bf16[512,256]{1,0:T(8,128)(2,1)S(1)}, u32[]{:S(2)}, u32[]{:S(2)}) collective-permute-start(bf16[512,256]{1,0:T(8,128)(2,1)} %get-tuple-element.51), channel_id=1, source_target_pairs={{0,8},{4,12},{8,16},{12,20},{16,24},{20,28},{24,0},{28,4},{1,9},{5... | collective-permute-start | bytes 786440 | tf_op jit(solution)/shard_map/cond/branch_0_fun/ppermute | solution.py:24
  68.0 3.7 %collective-permute-start.12 = (bf16[512,256]{1,0:T(8,128)(2,1)}, bf16[512,256]{1,0:T(8,128)(2,1)S(1)}, u32[]{:S(2)}, u32[]{:S(2)}) collective-permute-start(bf16[512,256]{1,0:T(8,128)(2,1)} %get-tuple-element.52), channel_id=1, source_target_pairs={{0,12},{4,16},{8,20},{12,24},{16,28},{20,0},{24,4},{28,8},{1,13},{... | collective-permute-start | bytes 786440 | tf_op jit(solution)/shard_map/cond/branch_0_fun/ppermute | solution.py:24
  71.7 6.6 %collective-permute-start.13 = (bf16[512,256]{1,0:T(8,128)(2,1)}, bf16[512,256]{1,0:T(8,128)(2,1)S(1)}, u32[]{:S(2)}, u32[]{:S(2)}) collective-permute-start(bf16[512,256]{1,0:T(8,128)(2,1)} %get-tuple-element.53), channel_id=1, source_target_pairs={{0,16},{4,20},{8,24},{12,28},{16,0},{20,4},{24,8},{28,12},{1,17},{... | collective-permute-start | bytes 786440 | tf_op jit(solution)/shard_map/cond/branch_0_fun/ppermute | solution.py:24
  78.3 3.4 %collective-permute-start.14 = (bf16[512,256]{1,0:T(8,128)(2,1)}, bf16[512,256]{1,0:T(8,128)(2,1)}, u32[]{:S(2)}, u32[]{:S(2)}) collective-permute-start(bf16[512,256]{1,0:T(8,128)(2,1)} %get-tuple-element.54), channel_id=1, source_target_pairs={{0,28},{4,0},{8,4},{12,8},{16,12},{20,16},{24,20},{28,24},{1,29},{... | collective-permute-start | bytes 786440 | tf_op jit(solution)/shard_map/cond/branch_0_fun/ppermute | solution.py:24
  81.8 3.4 %collective-permute-start.15 = (bf16[512,256]{1,0:T(8,128)(2,1)}, bf16[512,256]{1,0:T(8,128)(2,1)}, u32[]{:S(2)}, u32[]{:S(2)}) collective-permute-start(bf16[512,256]{1,0:T(8,128)(2,1)} %get-tuple-element.55), channel_id=1, source_target_pairs={{0,24},{4,28},{8,0},{12,4},{16,8},{20,12},{24,16},{28,20},{1,25},{... | collective-permute-start | bytes 786440 | tf_op jit(solution)/shard_map/cond/branch_0_fun/ppermute | solution.py:24
  85.1 6.6 %collective-permute-done.11.refs_2_ = bf16[512,256]{1,0:T(8,128)(2,1)S(1)} collective-permute-done((bf16[512,256]{1,0:T(8,128)(2,1)}, bf16[512,256]{1,0:T(8,128)(2,1)S(1)}, u32[]{:S(2)}, u32[]{:S(2)}) %collective-permute-start.11) | collective-permute-done | bytes 262176 | tf_op jit(solution)/shard_map/cond/branch_0_fun/ppermute | solution.py:24
  91.8 2.7 %collective-permute-start.16 = (bf16[512,256]{1,0:T(8,128)(2,1)}, bf16[512,256]{1,0:T(8,128)(2,1)}, u32[]{:S(2)}, u32[]{:S(2)}) collective-permute-start(bf16[512,256]{1,0:T(8,128)(2,1)} %get-tuple-element.56), channel_id=1, source_target_pairs={{0,20},{4,24},{8,28},{12,0},{16,4},{20,8},{24,12},{28,16},{1,21},{... | collective-permute-start | bytes 786440 | tf_op jit(solution)/shard_map/cond/branch_0_fun/ppermute | solution.py:24
  94.5 4.1 %forward.3 = bf16[4,128,512]{2,1,0:T(8,128)(2,1)} custom-call(bf16[512,2048]{1,0:T(8,128)(2,1)} %bitcast.61, bf16[256,512]{1,0:T(8,128)(2,1)S(1)} %bitcast.50, bf16[256,512]{1,0:T(8,128)(2,1)} %copy-done.21, bf16[256,512]{1,0:T(8,128)(2,1)} %copy-done.27, bf16[256,512]{1,0:T(8,128)(2,1)} %collective-permute-done.2.refs_3_, ...), custom_call_target="tpu_custom_call" | custom-call | flops 1073741824 | bytes 5242880 | tf_op jit(solution)/shard_map/cond/branch_0_fun/forward/pallas_call | solution.py:132
  98.6 4.8 %all-to-all-start.1 = ((bf16[4,128,512]{2,1,0:T(8,128)(2,1)}), bf16[4,128,512]{2,1,0:T(8,128)(2,1)S(1)}, u32[]{:S(2)}, u32[]{:S(2)}) async-start(bf16[4,128,512]{2,1,0:T(8,128)(2,1)} %forward.3), calls=%async_computation.1 | async-start | bytes 1048576 | tf_op jit(solution)/shard_map/cond/branch_0_fun/all_to_all | solution.py:231
  104.9 8.2 %collective-permute-done.15.refs_6_ = bf16[512,256]{1,0:T(8,128)(2,1)} collective-permute-done((bf16[512,256]{1,0:T(8,128)(2,1)}, bf16[512,256]{1,0:T(8,128)(2,1)}, u32[]{:S(2)}, u32[]{:S(2)}) %collective-permute-start.15) | collective-permute-done | bytes 262176 | tf_op jit(solution)/shard_map/cond/branch_0_fun/ppermute | solution.py:24
  113.1 11.3 %collective-permute-done.16.refs_7_ = bf16[512,256]{1,0:T(8,128)(2,1)} collective-permute-done((bf16[512,256]{1,0:T(8,128)(2,1)}, bf16[512,256]{1,0:T(8,128)(2,1)}, u32[]{:S(2)}, u32[]{:S(2)}) %collective-permute-start.16) | collective-permute-done | bytes 262176 | tf_op jit(solution)/shard_map/cond/branch_0_fun/ppermute | solution.py:24
  124.4 2.9 %update.3 = (f32[256,512]{1,0:T(8,128)}, f32[256,512]{1,0:T(8,128)}, bf16[256,512]{1,0:T(8,128)(2,1)}) custom-call(f32[2]{0:T(128)} %pad_maximum_fusion.2.bias_ref, f32[256,512]{1,0:T(8,128)S(1)} %bitcast.66, f32[256,512]{1,0:T(8,128)S(1)} %bitcast.69, bf16[256,512]{1,0:T(8,128)(2,1)S(1)} %bitcast.51, f32[512,256]{1,0:T(8,128)} %get-tuple-element.49.refs_0_, ...), custom_call_target="tpu_custom_call" | custom-call | flops 3932160 | bytes 4456448 | tf_op jit(solution)/shard_map/cond/branch_0_fun/update/pallas_call | solution.py:183
  127.2 4.7 %collective-permute-start.17 = (bf16[256,512]{1,0:T(8,128)(2,1)}, bf16[256,512]{1,0:T(8,128)(2,1)S(1)}, u32[]{:S(2)}, u32[]{:S(2)}) collective-permute-start(bf16[256,512]{1,0:T(8,128)(2,1)} %get-tuple-element.57), channel_id=1, source_target_pairs={{480,0},{0,32},{32,64},{64,96},{96,128},{128,160},{160,192},{192,2... | collective-permute-start | bytes 786440 | tf_op jit(solution)/shard_map/cond/branch_0_fun/ppermute | solution.py:239
  134.6 11.1 %collective-permute-done.17 = bf16[256,512]{1,0:T(8,128)(2,1)S(1)} collective-permute-done((bf16[256,512]{1,0:T(8,128)(2,1)}, bf16[256,512]{1,0:T(8,128)(2,1)S(1)}, u32[]{:S(2)}, u32[]{:S(2)}) %collective-permute-start.17) | collective-permute-done | bytes 262176 | tf_op jit(solution)/shard_map/cond/branch_0_fun/ppermute | solution.py:239
  (52 shorter events, 9.9 us)
Async XLA Ops:
  5.7 33.2 %copy-start.15 = (bf16[128,512]{1,0:T(8,128)(2,1)S(1)}, bf16[128,512]{1,0:T(8,128)(2,1)}, u32[]{:S(2)}) copy-start(bf16[128,512]{1,0:T(8,128)(2,1)} %get-tuple-element.48.values_ref) | copy-start | bytes 393220 | tf_op jit(solution)/shard_map/cond
  5.7 53.3 %all-to-all-start = ((bf16[4,128,2048]{2,1,0:T(8,128)(2,1)}), bf16[4,128,2048]{2,1,0:T(8,128)(2,1)S(1)}, u32[]{:S(2)}, u32[]{:S(2)}) async-start(bf16[4,128,2048]{2,1,0:T(8,128)(2,1)} %norm.3), calls=%async_computation | async-start | bytes 4194304 | tf_op jit(solution)/shard_map/cond/branch_0_fun/all_to_all | solution.py:209
  10.6 12.1 %collective-permute-start.3 = (bf16[256,512]{1,0:T(8,128)(2,1)S(1)}, bf16[256,512]{1,0:T(8,128)(2,1)S(1)}, u32[]{:S(2)}, u32[]{:S(2)}) collective-permute-start(bf16[256,512]{1,0:T(8,128)(2,1)S(1)} %bitcast.48), channel_id=1, source_target_pairs={{0,4},{4,8},{8,12},{12,16},{16,20},{20,24},{24,28},{28,0},{1,5},{5... | collective-permute-start | bytes 786440 | tf_op jit(solution)/shard_map/cond/branch_0_fun/ppermute | solution.py:24
  16.9 12.5 %collective-permute-start = (bf16[256,512]{1,0:T(8,128)(2,1)S(1)}, bf16[256,512]{1,0:T(8,128)(2,1)S(1)}, u32[]{:S(2)}, u32[]{:S(2)}) collective-permute-start(bf16[256,512]{1,0:T(8,128)(2,1)S(1)} %bitcast.49), channel_id=1, source_target_pairs={{0,28},{4,0},{8,4},{12,8},{16,12},{20,16},{24,20},{28,24},{1,29},{... | collective-permute-start | bytes 786440 | tf_op jit(solution)/shard_map/cond/branch_0_fun/ppermute | solution.py:24
  22.7 41.4 %copy-start.18 = (bf16[256,512]{1,0:T(8,128)(2,1)}, bf16[256,512]{1,0:T(8,128)(2,1)S(1)}, u32[]{:S(2)}) copy-start(bf16[256,512]{1,0:T(8,128)(2,1)S(1)} %collective-permute-done.3.refs_7_) | copy-start | bytes 786436 | tf_op jit(solution)/shard_map/cond
  22.7 10.6 %collective-permute-start.4 = (bf16[256,512]{1,0:T(8,128)(2,1)S(1)}, bf16[256,512]{1,0:T(8,128)(2,1)S(1)}, u32[]{:S(2)}, u32[]{:S(2)}) collective-permute-start(bf16[256,512]{1,0:T(8,128)(2,1)S(1)} %collective-permute-done.3.refs_7_), channel_id=1, source_target_pairs={{0,4},{4,8},{8,12},{12,16},{16,20},{20,24},{24,28},{28,0},{1,5},{5... | collective-permute-start | bytes 786440 | tf_op jit(solution)/shard_map/cond/branch_0_fun/ppermute | solution.py:24
  29.4 34.8 %copy-start.21 = (bf16[256,512]{1,0:T(8,128)(2,1)}, bf16[256,512]{1,0:T(8,128)(2,1)S(1)}, u32[]{:S(2)}) copy-start(bf16[256,512]{1,0:T(8,128)(2,1)S(1)} %collective-permute-done.refs_1_) | copy-start | bytes 786436 | tf_op jit(solution)/shard_map/cond
  29.4 22.5 %collective-permute-start.1 = (bf16[256,512]{1,0:T(8,128)(2,1)S(1)}, bf16[256,512]{1,0:T(8,128)(2,1)S(1)}, u32[]{:S(2)}, u32[]{:S(2)}) collective-permute-start(bf16[256,512]{1,0:T(8,128)(2,1)S(1)} %collective-permute-done.refs_1_), channel_id=1, source_target_pairs={{0,28},{4,0},{8,4},{12,8},{16,12},{20,16},{24,20},{28,24},{1,29},{... | collective-permute-start | bytes 786440 | tf_op jit(solution)/shard_map/cond/branch_0_fun/ppermute | solution.py:24
  33.3 61.2 %copy-start.24 = (bf16[256,512]{1,0:T(8,128)(2,1)}, bf16[256,512]{1,0:T(8,128)(2,1)S(1)}, u32[]{:S(2)}) copy-start(bf16[256,512]{1,0:T(8,128)(2,1)S(1)} %collective-permute-done.4.refs_6_) | copy-start | bytes 786436 | tf_op jit(solution)/shard_map/cond
  33.3 20.5 %collective-permute-start.5 = (bf16[256,512]{1,0:T(8,128)(2,1)S(1)}, bf16[256,512]{1,0:T(8,128)(2,1)}, u32[]{:S(2)}, u32[]{:S(2)}) collective-permute-start(bf16[256,512]{1,0:T(8,128)(2,1)S(1)} %collective-permute-done.4.refs_6_), channel_id=1, source_target_pairs={{0,4},{4,8},{8,12},{12,16},{16,20},{20,24},{24,28},{28,0},{1,5},{5... | collective-permute-start | bytes 786440 | tf_op jit(solution)/shard_map/cond/branch_0_fun/ppermute | solution.py:24
  40.7 8.6 %collective-permute-start.7 = (bf16[512,128]{1,0:T(8,128)(2,1)}, bf16[512,128]{1,0:T(8,128)(2,1)S(1)}, u32[]{:S(2)}, u32[]{:S(2)}) collective-permute-start(bf16[512,128]{1,0:T(8,128)(2,1)} %turn_back.3.d00), channel_id=1, source_target_pairs={{0,2},{2,0},{1,3},{3,1},{4,6},{6,4},{5,7},{7,5},{8,10},{10,8},{9,1... | collective-permute-start | bytes 393224 | tf_op jit(solution)/shard_map/cond/branch_0_fun/ppermute | solution.py:28
  43.3 15.6 %collective-permute-start.8 = (bf16[512,128]{1,0:T(8,128)(2,1)}, bf16[512,128]{1,0:T(8,128)(2,1)}, u32[]{:S(2)}, u32[]{:S(2)}) collective-permute-start(bf16[512,128]{1,0:T(8,128)(2,1)} %turn_back.3.d00), channel_id=1, source_target_pairs={{0,1},{1,0},{2,3},{3,2},{4,5},{5,4},{6,7},{7,6},{8,9},{9,8},{10,11... | collective-permute-start | bytes 393224 | tf_op jit(solution)/shard_map/cond/branch_0_fun/ppermute | solution.py:28
  49.3 9.7 %copy-start.42 = (bf16[512,128]{1,0:T(8,128)(2,1)}, bf16[512,128]{1,0:T(8,128)(2,1)S(1)}, u32[]{:S(2)}) copy-start(bf16[512,128]{1,0:T(8,128)(2,1)S(1)} %collective-permute-done.7.d10) | copy-start | bytes 393220 | tf_op jit(solution)/shard_map/cond
  49.3 9.7 %collective-permute-start.9 = (bf16[512,128]{1,0:T(8,128)(2,1)S(1)}, bf16[512,128]{1,0:T(8,128)(2,1)}, u32[]{:S(2)}, u32[]{:S(2)}) collective-permute-start(bf16[512,128]{1,0:T(8,128)(2,1)S(1)} %collective-permute-done.7.d10), channel_id=1, source_target_pairs={{0,1},{1,0},{2,3},{3,2},{4,5},{5,4},{6,7},{7,6},{8,9},{9,8},{10,11... | collective-permute-start | bytes 393224 | tf_op jit(solution)/shard_map/cond/branch_0_fun/ppermute | solution.py:28
  51.8 42.7 %copy-start.27 = (bf16[256,512]{1,0:T(8,128)(2,1)}, bf16[256,512]{1,0:T(8,128)(2,1)S(1)}, u32[]{:S(2)}) copy-start(bf16[256,512]{1,0:T(8,128)(2,1)S(1)} %collective-permute-done.1.refs_2_) | copy-start | bytes 786436 | tf_op jit(solution)/shard_map/cond
  51.8 19.8 %collective-permute-start.2 = (bf16[256,512]{1,0:T(8,128)(2,1)S(1)}, bf16[256,512]{1,0:T(8,128)(2,1)}, u32[]{:S(2)}, u32[]{:S(2)}) collective-permute-start(bf16[256,512]{1,0:T(8,128)(2,1)S(1)} %collective-permute-done.1.refs_2_), channel_id=1, source_target_pairs={{0,28},{4,0},{8,4},{12,8},{16,12},{20,16},{24,20},{28,24},{1,29},{... | collective-permute-start | bytes 786440 | tf_op jit(solution)/shard_map/cond/branch_0_fun/ppermute | solution.py:24
  53.8 24.6 %collective-permute-start.6 = (bf16[256,512]{1,0:T(8,128)(2,1)}, bf16[256,512]{1,0:T(8,128)(2,1)}, u32[]{:S(2)}, u32[]{:S(2)}) collective-permute-start(bf16[256,512]{1,0:T(8,128)(2,1)} %collective-permute-done.5.refs_5_), channel_id=1, source_target_pairs={{0,4},{4,8},{8,12},{12,16},{16,20},{20,24},{24,28},{28,0},{1,5},{5... | collective-permute-start | bytes 786440 | tf_op jit(solution)/shard_map/cond/branch_0_fun/ppermute | solution.py:24
  64.2 17.6 %collective-permute-start.10 = (bf16[512,256]{1,0:T(8,128)(2,1)}, bf16[512,256]{1,0:T(8,128)(2,1)S(1)}, u32[]{:S(2)}, u32[]{:S(2)}) collective-permute-start(bf16[512,256]{1,0:T(8,128)(2,1)} %get-tuple-element.50), channel_id=1, source_target_pairs={{0,4},{4,8},{8,12},{12,16},{16,20},{20,24},{24,28},{28,0},{1,5},{5... | collective-permute-start | bytes 786440 | tf_op jit(solution)/shard_map/cond/branch_0_fun/ppermute | solution.py:24
  66.1 25.7 %collective-permute-start.11 = (bf16[512,256]{1,0:T(8,128)(2,1)}, bf16[512,256]{1,0:T(8,128)(2,1)S(1)}, u32[]{:S(2)}, u32[]{:S(2)}) collective-permute-start(bf16[512,256]{1,0:T(8,128)(2,1)} %get-tuple-element.51), channel_id=1, source_target_pairs={{0,8},{4,12},{8,16},{12,20},{16,24},{20,28},{24,0},{28,4},{1,9},{5... | collective-permute-start | bytes 786440 | tf_op jit(solution)/shard_map/cond/branch_0_fun/ppermute | solution.py:24
  68.0 36.8 %collective-permute-start.12 = (bf16[512,256]{1,0:T(8,128)(2,1)}, bf16[512,256]{1,0:T(8,128)(2,1)S(1)}, u32[]{:S(2)}, u32[]{:S(2)}) collective-permute-start(bf16[512,256]{1,0:T(8,128)(2,1)} %get-tuple-element.52), channel_id=1, source_target_pairs={{0,12},{4,16},{8,20},{12,24},{16,28},{20,0},{24,4},{28,8},{1,13},{... | collective-permute-start | bytes 786440 | tf_op jit(solution)/shard_map/cond/branch_0_fun/ppermute | solution.py:24
  71.7 33.2 %collective-permute-start.13 = (bf16[512,256]{1,0:T(8,128)(2,1)}, bf16[512,256]{1,0:T(8,128)(2,1)S(1)}, u32[]{:S(2)}, u32[]{:S(2)}) collective-permute-start(bf16[512,256]{1,0:T(8,128)(2,1)} %get-tuple-element.53), channel_id=1, source_target_pairs={{0,16},{4,20},{8,24},{12,28},{16,0},{20,4},{24,8},{28,12},{1,17},{... | collective-permute-start | bytes 786440 | tf_op jit(solution)/shard_map/cond/branch_0_fun/ppermute | solution.py:24
  78.3 26.5 %collective-permute-start.14 = (bf16[512,256]{1,0:T(8,128)(2,1)}, bf16[512,256]{1,0:T(8,128)(2,1)}, u32[]{:S(2)}, u32[]{:S(2)}) collective-permute-start(bf16[512,256]{1,0:T(8,128)(2,1)} %get-tuple-element.54), channel_id=1, source_target_pairs={{0,28},{4,0},{8,4},{12,8},{16,12},{20,16},{24,20},{28,24},{1,29},{... | collective-permute-start | bytes 786440 | tf_op jit(solution)/shard_map/cond/branch_0_fun/ppermute | solution.py:24
  81.7 16.9 %copy-start.30 = (bf16[512,256]{1,0:T(8,128)(2,1)}, bf16[512,256]{1,0:T(8,128)(2,1)S(1)}, u32[]{:S(2)}) copy-start(bf16[512,256]{1,0:T(8,128)(2,1)S(1)} %collective-permute-done.10.refs_1_) | copy-start | bytes 786436 | tf_op jit(solution)/shard_map/cond
  81.8 31.3 %collective-permute-start.15 = (bf16[512,256]{1,0:T(8,128)(2,1)}, bf16[512,256]{1,0:T(8,128)(2,1)}, u32[]{:S(2)}, u32[]{:S(2)}) collective-permute-start(bf16[512,256]{1,0:T(8,128)(2,1)} %get-tuple-element.55), channel_id=1, source_target_pairs={{0,24},{4,28},{8,0},{12,4},{16,8},{20,12},{24,16},{28,20},{1,25},{... | collective-permute-start | bytes 786440 | tf_op jit(solution)/shard_map/cond/branch_0_fun/ppermute | solution.py:24
  91.8 6.9 %copy-start.33 = (bf16[512,256]{1,0:T(8,128)(2,1)}, bf16[512,256]{1,0:T(8,128)(2,1)S(1)}, u32[]{:S(2)}) copy-start(bf16[512,256]{1,0:T(8,128)(2,1)S(1)} %collective-permute-done.11.refs_2_) | copy-start | bytes 786436 | tf_op jit(solution)/shard_map/cond
  91.8 32.6 %copy-start.6 = (f32[1,256,512]{2,1,0:T(8,128)S(1)}, f32[1,256,512]{2,1,0:T(8,128)}, u32[]{:S(2)}) copy-start(f32[1,256,512]{2,1,0:T(8,128)} %get-tuple-element.46) | copy-start | bytes 1572868 | tf_op jit(solution)/shard_map/cond
  91.8 32.6 %copy-start.9 = (f32[1,256,512]{2,1,0:T(8,128)S(1)}, f32[1,256,512]{2,1,0:T(8,128)}, u32[]{:S(2)}) copy-start(f32[1,256,512]{2,1,0:T(8,128)} %get-tuple-element.47) | copy-start | bytes 1572868 | tf_op jit(solution)/shard_map/cond
  91.8 32.6 %collective-permute-start.16 = (bf16[512,256]{1,0:T(8,128)(2,1)}, bf16[512,256]{1,0:T(8,128)(2,1)}, u32[]{:S(2)}, u32[]{:S(2)}) collective-permute-start(bf16[512,256]{1,0:T(8,128)(2,1)} %get-tuple-element.56), channel_id=1, source_target_pairs={{0,20},{4,24},{8,28},{12,0},{16,4},{20,8},{24,12},{28,16},{1,21},{... | collective-permute-start | bytes 786440 | tf_op jit(solution)/shard_map/cond/branch_0_fun/ppermute | solution.py:24
  98.6 33.3 %all-to-all-start.1 = ((bf16[4,128,512]{2,1,0:T(8,128)(2,1)}), bf16[4,128,512]{2,1,0:T(8,128)(2,1)S(1)}, u32[]{:S(2)}, u32[]{:S(2)}) async-start(bf16[4,128,512]{2,1,0:T(8,128)(2,1)} %forward.3), calls=%async_computation.1 | async-start | bytes 1048576 | tf_op jit(solution)/shard_map/cond/branch_0_fun/all_to_all | solution.py:231
  104.8 19.5 %copy-start.36 = (bf16[512,256]{1,0:T(8,128)(2,1)}, bf16[512,256]{1,0:T(8,128)(2,1)S(1)}, u32[]{:S(2)}) copy-start(bf16[512,256]{1,0:T(8,128)(2,1)S(1)} %collective-permute-done.12.refs_3_) | copy-start | bytes 786436 | tf_op jit(solution)/shard_map/cond
  104.8 19.5 %copy-start.39 = (bf16[512,256]{1,0:T(8,128)(2,1)}, bf16[512,256]{1,0:T(8,128)(2,1)S(1)}, u32[]{:S(2)}) copy-start(bf16[512,256]{1,0:T(8,128)(2,1)S(1)} %collective-permute-done.13.refs_4_) | copy-start | bytes 786436 | tf_op jit(solution)/shard_map/cond
  127.2 18.5 %collective-permute-start.17 = (bf16[256,512]{1,0:T(8,128)(2,1)}, bf16[256,512]{1,0:T(8,128)(2,1)S(1)}, u32[]{:S(2)}, u32[]{:S(2)}) collective-permute-start(bf16[256,512]{1,0:T(8,128)(2,1)} %get-tuple-element.57), channel_id=1, source_target_pairs={{480,0},{0,32},{32,64},{64,96},{96,128},{128,160},{160,192},{192,2... | collective-permute-start | bytes 786440 | tf_op jit(solution)/shard_map/cond/branch_0_fun/ppermute | solution.py:239
  (3 other events, 7.0 us)
where the time goes:
time: 149 us; the launch traced here: 147 us
  starting transfers between devices  72.8 us (49%)
  waiting for transfers between devices  47.1 us (32%)
  Pallas kernels  18.9 us (13%)
  other arithmetic  4.12 us (3%)
  local copies, waits for them, and re-layouts  2.11 us (1%)
    ppermute x14, starting transfers between devices, shifted(): lax.ppermute(block, 'y', [(i, (i + distance) % NY) for i in range(NY)])  51.9 us
    ppermute x14, waiting for transfers between devices, shifted(): lax.ppermute(block, 'y', [(i, (i + distance) % NY) for i in range(NY)])  32 us
    ppermute x1, waiting for transfers between devices, one_distance(): lax.ppermute(local, 'rep', [((i - distance) % groups, i) for i in range(g...  11.1 us
    ppermute x3, starting transfers between devices, across(): return lax.ppermute(block, axis, [(0, 1), (1, 0)])  6.45 us
    all_to_all x1, starting transfers between devices, one_distance(): lax.all_to_all(tokens, PLANE, 0, 0, tiled=True).reshape(NP * rows, -1)  4.93 us
    all_to_all x1, starting transfers between devices, one_distance(): parts = lax.all_to_all(parts, PLANE, 0, 0, tiled=True)  4.8 us
    ppermute x1, starting transfers between devices, one_distance(): lax.ppermute(local, 'rep', [((i - distance) % groups, i) for i in range(g...  4.68 us
    pallas_call x1, Pallas kernels, norm(): pl.pallas_call(norm_kernel, grid=(rows // step,), in_specs=[SMEM, pl.Bloc...  4.34 us
  transfers between devices with their start and end apart: 20, of which 7 were waited for; matrix products, arithmetic and copies ran while one was open for 2% of the time, Pallas kernels for 10%

commit v1 on v0

--- a/solution.py
+++ b/solution.py
@@ -11,17 +11,26 @@
 
 
 HEAD = 128
-NY, NP = 8, 4
-GROUP = ("y", "x", "c")
-PLANE = ("x", "c")
-EVERY = ("rep", "y", "x", "c")
+NY, NP = 4, 8
+GROUP = ("y", "h", "x", "c")
+PLANE = ("h", "x", "c")
+EVERY = ("rep", "y", "h", "x", "c")
 DISTANCES = (1, 2, 4)
-SENDS = (1, 2, 3, 4, 7, 6, 5)
+SENDS = (1, 3, 2)
 BF16, F32 = jnp.bfloat16, jnp.float32
 
 
 def shifted(block, distance):
     return lax.ppermute(block, "y", [(i, (i + distance) % NY) for i in range(NY)])
+
+
+def toward(block):
+    route = []
+    for y in range(NY):
+        for c in range(2):
+            sender = (y + 1 if c == 0 else y - 1) % NY
+            route.append((sender * 2 + c, y * 2 + c))
+    return lax.ppermute(block, ("y", "c"), route)
 
 
 def across(block, axis):
@@ -70,73 +79,77 @@
     )(y, hidden, gain)
 
 
-def turn_back_kernel(values_ref, cosine_ref, sine_ref, out_ref):
-    for h in range(values_ref.shape[1] // HEAD):
-        cols = slice(h * HEAD, (h + 1) * HEAD)
-        turned = turn(values_ref[:, cols].astype(F32), cosine_ref[...], -sine_ref[...])
-        out_ref[cols, :] = turned.T.astype(BF16)
-
-
-def turn_back(values, cosine, sine):
+def turn_back_kernel(at_ref, own_ref, beside_ref, two_ref, four_ref, cosine_ref, sine_ref, out_ref):
+    pieces = [own_ref, beside_ref, *(two_ref.at[i] for i in range(2)), *(four_ref.at[i] for i in range(4))]
+    rows, kvw = own_ref.shape
+    for i, piece in enumerate(pieces):
+        start = pl.multiple_of(at_ref[i] * rows, 128)
+        cosine, sine = cosine_ref[pl.ds(start, rows), :], sine_ref[pl.ds(start, rows), :]
+        for h in range(kvw // HEAD):
+            cols = slice(h * HEAD, (h + 1) * HEAD)
+            turned = turn(piece[:, cols].astype(F32), cosine, -sine)
+            out_ref[cols, pl.ds(start, rows)] = turned.T.astype(BF16)
+
+
+def turn_back(at, pieces, cosine, sine):
+    rows, kvw = pieces[0].shape
     return pl.pallas_call(
         turn_back_kernel,
-        in_specs=vmem(3),
+        in_specs=[SMEM] + vmem(len(pieces) + 2),
         out_specs=pl.BlockSpec(memory_space=pltpu.VMEM),
-        out_shape=jax.ShapeDtypeStruct(values.shape[::-1], BF16),
-        cost_estimate=cost(4 * values.size, 4 * values.size),
+        out_shape=jax.ShapeDtypeStruct((kvw, NP * rows), BF16),
+        cost_estimate=cost(8 * NP * rows * kvw, 6 * NP * rows * kvw),
         name="turn_back",
-    )(values, cosine, sine)
-
-
-def grads_kernel(at_ref, tokens_ref, d00, d10, d01, d11, *refs):
-    outs, dpre_ref = refs[:-1], refs[-1]
-    rows = d00.shape[1]
-    for i, piece in enumerate((d00, d10, d01, d11)):
-        dpre_ref[:, pl.ds(pl.multiple_of(at_ref[i] * rows, 128), rows)] = piece[...]
+    )(at, *pieces, cosine, sine)
+
+
+def grads_kernel(tokens_ref, dpre_ref, *outs):
     feat = outs[0].shape[1]
     for k, out in enumerate(outs):
         block = tokens_ref[:, k * feat : (k + 1) * feat]
         out[...] = jnp.dot(dpre_ref[...], block, preferred_element_type=F32).astype(out.dtype)
 
 
-def grads(at, tokens, pieces):
+def grads(tokens, dpre):
     count, width = tokens.shape
-    kvw = pieces[0].shape[0]
+    kvw = dpre.shape[0]
     feat = width // NY
     return pl.pallas_call(
         grads_kernel,
-        in_specs=[SMEM] + vmem(1 + len(pieces)),
+        in_specs=vmem(2),
         out_specs=vmem(NY),
         out_shape=[jax.ShapeDtypeStruct((kvw, feat), BF16 if k else F32) for k in range(NY)],
-        scratch_shapes=[pltpu.VMEM((kvw, count), BF16)],
         cost_estimate=cost(2 * count * width * kvw, 2 * count * width + 3 * width * kvw),
         name="grads",
-    )(at, tokens, *pieces)
-
-
-def forward_kernel(tokens_ref, *refs):
-    weights, out_ref = refs[:-1], refs[-1]
-    feat = weights[0].shape[0]
+    )(tokens, dpre)
+
+
+def forward_kernel(core_ref, tokens_ref, w0, w2, pair_ref, out_ref):
+    feat = w0.shape[0]
     rows = out_ref.shape[1]
+    here = pl.multiple_of((1 + 2 * core_ref[0]) * feat, 128)
+    there = pl.multiple_of((3 - 2 * core_ref[0]) * feat, 128)
     for p in range(NP):
         mine = slice(p * rows, (p + 1) * rows)
-        total = jnp.zeros(out_ref.shape[1:], F32)
-        for k, weight in enumerate(weights):
-            total += jnp.dot(tokens_ref[mine, k * feat : (k + 1) * feat], weight[...], preferred_element_type=F32)
+
+        def term(start, weight):
+            return jnp.dot(tokens_ref[mine, pl.ds(start, feat)], weight, preferred_element_type=F32)
+
+        total = term(0, w0[...]) + term(2 * feat, w2[...]) + term(here, pair_ref[0]) + term(there, pair_ref[1])
         out_ref[p] = total.astype(out_ref.dtype)
 
 
-def forward(tokens, weights):
+def forward(core, tokens, weights):
     count, width = tokens.shape
     kvw = weights[0].shape[1]
     return pl.pallas_call(
         forward_kernel,
-        in_specs=vmem(1 + len(weights)),
+        in_specs=[SMEM] + vmem(1 + len(weights)),
         out_specs=pl.BlockSpec(memory_space=pltpu.VMEM),
         out_shape=jax.ShapeDtypeStruct((NP, count // NP, kvw), BF16),
         cost_estimate=cost(2 * count * width * kvw, 5 << 20),
         name="forward",
-    )(tokens, *weights)
+    )(core, tokens, *weights)
 
 
 def keys_kernel(scale, parts_ref, cosine_ref, sine_ref, out_ref):
@@ -203,31 +216,30 @@
     rows, width = hidden.shape
     scale = width ** (-0.5)
     weight = key_weight[0]
-    y, x, c = [lax.axis_index(axis).astype(jnp.int32) for axis in GROUP]
-
+    y, h, x, c = [lax.axis_index(axis).astype(jnp.int32) for axis in GROUP]
+
+    beside = across(dkeys, "h")
     tokens = norm(y.reshape(1), hidden, gain.reshape(1, -1))
+    two = across(jnp.stack([dkeys, beside]), "x")
     tokens = lax.all_to_all(tokens, PLANE, 0, 0, tiled=True).reshape(NP * rows, -1)
-
-    positions = lax.axis_index(GROUP) * rows + jnp.arange(rows)
-    cosine, sine = rotation(positions)
-    own = turn_back(dkeys, cosine, sine)
-    beside = across(own, "x")
-    other = across(own, "c")
-    corner = across(beside, "c")
-
-    held = {0: weight}
-    for k in (1, 2, 3, 4):
-        held[NY - k] = shifted(held[(NY + 1 - k) % NY], 1)
-        if k < 4:
-            held[k] = shifted(held[k - 1], -1)
-
-    at = jnp.stack([x * 2 + c, (1 - x) * 2 + c, x * 2 + 1 - c, (1 - x) * 2 + 1 - c])
-    blocks = grads(at, tokens, (own, beside, other, corner))
+    four = across(jnp.concatenate([jnp.stack([dkeys, beside]), two]), "c")
+    cosine, sine = rotation(y * NP * rows + jnp.arange(NP * rows))
+    at = jnp.stack(
+        [(h ^ dh) * 4 + (x ^ dx) * 2 + (c ^ dc) for dc in (0, 1) for dx in (0, 1) for dh in (0, 1)]
+    )
+    dpre = turn_back(at, (dkeys, beside, two, four), cosine, sine)
+    start = at[0] * rows
+    cosine, sine = [lax.dynamic_slice_in_dim(table, start, rows) for table in (cosine, sine)]
+
+    w2 = shifted(weight, 2)
+    pair = toward(jnp.stack([weight, w2]))
+
+    blocks = grads(tokens, dpre)
     arrived = [blocks[0]]
     for k in SENDS:
         arrived.append(shifted(blocks[k], k))
 
-    parts = forward(tokens, [held[k] for k in range(NY)])
+    parts = forward(c.reshape(1), tokens, (weight, w2, pair))
     parts = lax.all_to_all(parts, PLANE, 0, 0, tiled=True)
     keys = finish_keys(parts, cosine, sine, scale)
 
@@ -252,7 +264,7 @@
 
 
 def solution(mesh):
-    finer = Mesh(mesh.devices.reshape(mesh.shape["rep"], NY, 2, 2), EVERY)
+    finer = Mesh(mesh.devices.reshape(mesh.shape["rep"], NY, 2, 2, 2), EVERY)
     placed = (
         P(EVERY, None),
         P(),

time: 149 us -> 158 us (1.060)
  the two profiles are of different devices: /device:TPU:60 before, /device:TPU:12 now
where the time goes in v1:
time: 158 us; the launch traced here: 157 us
  waiting for transfers between devices  77.4 us (49%)
  starting transfers between devices  47.8 us (30%)
  Pallas kernels  20.6 us (13%)
  other arithmetic  7.34 us (5%)
  local copies, waits for them, and re-layouts  2 us (1%)
    ppermute x4, waiting for transfers between devices, shifted(): lax.ppermute(block, 'y', [(i, (i + distance) % NY) for i in range(NY)])  52.1 us
    ppermute x4, starting transfers between devices, shifted(): lax.ppermute(block, 'y', [(i, (i + distance) % NY) for i in range(NY)])  17.7 us
    ppermute x3, waiting for transfers between devices, across(): return lax.ppermute(block, axis, [(0, 1), (1, 0)])  12.8 us
    ppermute x1, waiting for transfers between devices, one_distance(): lax.ppermute(local, 'rep', [((i - distance) % groups, i) for i in range(g...  12.4 us
    all_to_all x1, starting transfers between devices, one_distance(): lax.all_to_all(tokens, PLANE, 0, 0, tiled=True).reshape(NP * rows, -1)  9.41 us
    all_to_all x1, starting transfers between devices, one_distance(): parts = lax.all_to_all(parts, PLANE, 0, 0, tiled=True)  9 us
    ppermute x3, starting transfers between devices, across(): return lax.ppermute(block, axis, [(0, 1), (1, 0)])  7.01 us
    pallas_call x1, Pallas kernels, norm(): pl.pallas_call(norm_kernel, grid=(rows // step,), in_specs=[SMEM, pl.Bloc...  4.32 us
  transfers between devices with their start and end apart: 11, of which 6 were waited for; matrix products, arithmetic and copies ran while one was open for 5% of the time, Pallas kernels for 9%

profile of v1, /device:TPU:12, one launch (start us, length us, event | category | flops | bytes accessed | tf_op | source)
XLA Modules:
  0.0 157.4 jit_solution(13543282923844482790)
XLA Ops:
  1.3 156.1 %conditional.1 = (bf16[128,512]{1,0:T(8,128)(2,1)}, bf16[1,256,512]{2,1,0:T(8,128)(2,1)}, f32[1,256,512]{2,1,0:T(8,128)}, f32[1,256,512]{2,1,0:T(8,128)}) conditional(s32[]{:T(128)} %clamp.3, (f32[8192]{0:T(1024)}, bf16[128,8192]{1,0:T(8,128)(2,1)}, bf16[1,256,512]{2,1,0:T(8,128)(2,1)}, s32[]{:T(128)}, f32[1,256,512]{2,1,0:T(8,128)}, ...), branch_computations={%region_0.1_spmd, %region_1.2_spmd, %region_2.3_spmd} | conditional | flops 2168096768 | bytes 68036368 | solution.py:263
  1.3 4.3 %norm.3 = bf16[8,128,1024]{2,1,0:T(8,128)(2,1)} custom-call(s32[1]{0:T(128)} %bitcast.1.y_ref, bf16[128,8192]{1,0:T(8,128)(2,1)} %get-tuple-element.42.rows_ref, f32[1,8192]{1,0:T(1,128)} %bitcast.108), custom_call_target="tpu_custom_call" | custom-call | flops 6291456 | bytes 4194304 | tf_op jit(solution)/shard_map/cond/branch_0_fun/norm/pallas_call | solution.py:71
  5.6 9.4 %all-to-all-start = ((bf16[8,128,1024]{2,1,0:T(8,128)(2,1)}), bf16[8,128,1024]{2,1,0:T(8,128)(2,1)S(1)}, u32[]{:S(2)}, u32[]{:S(2)}) async-start(bf16[8,128,1024]{2,1,0:T(8,128)(2,1)} %norm.3), calls=%async_computation | async-start | bytes 4194304 | tf_op jit(solution)/shard_map/cond/branch_0_fun/all_to_all | solution.py:224
  15.1 3.2 %collective-permute-start = (bf16[256,512]{1,0:T(8,128)(2,1)S(1)}, bf16[256,512]{1,0:T(8,128)(2,1)S(1)}, u32[]{:S(2)}, u32[]{:S(2)}) collective-permute-start(bf16[256,512]{1,0:T(8,128)(2,1)S(1)} %bitcast.72), channel_id=1, source_target_pairs={{0,16},{8,24},{16,0},{24,8},{1,17},{9,25},{17,1},{25,9},{2,18},{10... | collective-permute-start | bytes 786440 | tf_op jit(solution)/shard_map/cond/branch_0_fun/ppermute | solution.py:24
  18.3 33.0 %collective-permute-done.w2 = bf16[256,512]{1,0:T(8,128)(2,1)S(1)} collective-permute-done((bf16[256,512]{1,0:T(8,128)(2,1)S(1)}, bf16[256,512]{1,0:T(8,128)(2,1)S(1)}, u32[]{:S(2)}, u32[]{:S(2)}) %collective-permute-start) | collective-permute-done | bytes 262176 | tf_op jit(solution)/shard_map/cond/branch_0_fun/ppermute | solution.py:24
  51.3 0.9 pad_maximum_fusion
  52.2 1.9 %collective-permute-start.1 = (bf16[2,256,512]{2,1,0:T(8,128)(2,1)}, bf16[2,256,512]{2,1,0:T(8,128)(2,1)}, u32[]{:S(2)}, u32[]{:S(2)}) collective-permute-start(bf16[2,256,512]{2,1,0:T(8,128)(2,1)} %pad_maximum_fusion), channel_id=1, source_target_pairs={{8,0},{25,1},{16,8},{1,9},{24,16},{9,17},{0,24},{17,25},{10,2},{27... | collective-permute-start | bytes 1572872 | tf_op jit(solution)/shard_map/cond/branch_0_fun/ppermute | solution.py:33
  54.1 2.5 %collective-permute-start.2 = (bf16[128,512]{1,0:T(8,128)(2,1)S(1)}, bf16[128,512]{1,0:T(8,128)(2,1)S(1)}, u32[]{:S(2)}, u32[]{:S(2)}) collective-permute-start(bf16[128,512]{1,0:T(8,128)(2,1)S(1)} %copy-done.3), channel_id=1, source_target_pairs={{0,4},{4,0},{1,5},{5,1},{2,6},{6,2},{3,7},{7,3},{8,12},{12,8},{9,1... | collective-permute-start | bytes 393224 | tf_op jit(solution)/shard_map/cond/branch_0_fun/ppermute | solution.py:37
  56.6 12.8 %collective-permute-done.2.beside_ref = bf16[128,512]{1,0:T(8,128)(2,1)S(1)} collective-permute-done((bf16[128,512]{1,0:T(8,128)(2,1)S(1)}, bf16[128,512]{1,0:T(8,128)(2,1)S(1)}, u32[]{:S(2)}, u32[]{:S(2)}) %collective-permute-start.2) | collective-permute-done | bytes 131104 | tf_op jit(solution)/shard_map/cond/branch_0_fun/ppermute | solution.py:37
  69.5 2.5 %collective-permute-start.3 = (bf16[2,128,512]{2,1,0:T(8,128)(2,1)S(1)}, bf16[2,128,512]{2,1,0:T(8,128)(2,1)S(1)}, u32[]{:S(2)}, u32[]{:S(2)}) collective-permute-start(bf16[2,128,512]{2,1,0:T(8,128)(2,1)S(1)} %pad_maximum_fusion.4), channel_id=1, source_target_pairs={{0,2},{2,0},{1,3},{3,1},{4,6},{6,4},{5,7},{7,5},{8,10},{10,8},{9,1... | collective-permute-start | bytes 786440 | tf_op jit(solution)/shard_map/cond/branch_0_fun/ppermute | solution.py:37
  72.0 1.3 copy-done.6
  73.3 4.1 %forward.3 = bf16[8,128,512]{2,1,0:T(8,128)(2,1)} custom-call(s32[1]{0:T(128)} %bitcast.core_ref, bf16[1024,1024]{1,0:T(8,128)(2,1)} %bitcast.87, bf16[256,512]{1,0:T(8,128)(2,1)S(1)} %bitcast.73, bf16[256,512]{1,0:T(8,128)(2,1)} %copy-done.18, bf16[2,256,512]{2,1,0:T(8,128)(2,1)} %collective-permute-done.1.pair_ref), custom_call_target="tpu_custom_call" | custom-call | flops 1073741824 | bytes 5242880 | tf_op jit(solution)/shard_map/cond/branch_0_fun/forward/pallas_call | solution.py:145
  77.4 9.0 %all-to-all-start.1 = ((bf16[8,128,512]{2,1,0:T(8,128)(2,1)}), bf16[8,128,512]{2,1,0:T(8,128)(2,1)}, u32[]{:S(2)}, u32[]{:S(2)}) async-start(bf16[8,128,512]{2,1,0:T(8,128)(2,1)} %forward.3), calls=%async_computation.1 | async-start | bytes 2097152 | tf_op jit(solution)/shard_map/cond/branch_0_fun/all_to_all | solution.py:243
  86.5 2.0 %collective-permute-start.4 = (bf16[4,128,512]{2,1,0:T(8,128)(2,1)S(1)}, bf16[4,128,512]{2,1,0:T(8,128)(2,1)}, u32[]{:S(2)}, u32[]{:S(2)}) collective-permute-start(bf16[4,128,512]{2,1,0:T(8,128)(2,1)S(1)} %pad_maximum_fusion.1), channel_id=1, source_target_pairs={{0,1},{1,0},{2,3},{3,2},{4,5},{5,4},{6,7},{7,6},{8,9},{9,8},{10,11... | collective-permute-start | bytes 1572872 | tf_op jit(solution)/shard_map/cond/branch_0_fun/ppermute | solution.py:37
  88.5 0.7 stack.121.at_ref
  89.2 1.9 %multiply_sine_fusion = (f32[1024,64]{1,0:T(8,128)S(1)}, f32[1024,64]{1,0:T(8,128)S(1)}, f32[1024,64]{1,0:T(8,128)S(1)}) fusion(f32[64]{0:T(128)S(1)} %multiply_exponential_fusion, f32[1024]{0:T(1024)S(1)} %add_convert_fusion), kind=kLoop, calls=%fused_computation | loop fusion | flops 131072 | bytes 790784 | tf_op jit(solution)/shard_map/cond/branch_0_fun/sin | solution.py:211
  91.1 1.3 pad_maximum_fusion.2
  92.4 3.5 %turn_back.3.dpre_ref = bf16[512,1024]{1,0:T(8,128)(2,1)} custom-call(s32[8]{0:T(128)} %stack.121.at_ref, bf16[128,512]{1,0:T(8,128)(2,1)S(1)} %copy-done.3, bf16[128,512]{1,0:T(8,128)(2,1)} %copy-done.15, bf16[2,128,512]{2,1,0:T(8,128)(2,1)} %copy-done.21, bf16[4,128,512]{2,1,0:T(8,128)(2,1)} %collective-permute-done.4.four_ref, ...), custom_call_target="tpu_custom_call" | custom-call | flops 4194304 | bytes 3145728 | tf_op jit(solution)/shard_map/cond/branch_0_fun/turn_back/pallas_call | solution.py:96
  95.9 4.0 %grads.3 = (f32[512,256]{1,0:T(8,128)}, bf16[512,256]{1,0:T(8,128)(2,1)}, bf16[512,256]{1,0:T(8,128)(2,1)}, bf16[512,256]{1,0:T(8,128)(2,1)}) custom-call(bf16[1024,1024]{1,0:T(8,128)(2,1)} %bitcast.88, bf16[512,1024]{1,0:T(8,128)(2,1)} %turn_back.3.dpre_ref), custom_call_target="tpu_custom_call" | custom-call | flops 1073741824 | bytes 3670016 | tf_op jit(solution)/shard_map/cond/branch_0_fun/grads/pallas_call | solution.py:117
  99.9 4.8 %collective-permute-start.5 = (bf16[512,256]{1,0:T(8,128)(2,1)}, bf16[512,256]{1,0:T(8,128)(2,1)S(1)}, u32[]{:S(2)}, u32[]{:S(2)}) collective-permute-start(bf16[512,256]{1,0:T(8,128)(2,1)} %get-tuple-element.50), channel_id=1, source_target_pairs={{0,8},{8,16},{16,24},{24,0},{1,9},{9,17},{17,25},{25,1},{2,10},{10... | collective-permute-start | bytes 786440 | tf_op jit(solution)/shard_map/cond/branch_0_fun/ppermute | solution.py:24
  104.7 3.1 %collective-permute-start.6 = (bf16[512,256]{1,0:T(8,128)(2,1)}, bf16[512,256]{1,0:T(8,128)(2,1)S(1)}, u32[]{:S(2)}, u32[]{:S(2)}) collective-permute-start(bf16[512,256]{1,0:T(8,128)(2,1)} %get-tuple-element.51), channel_id=1, source_target_pairs={{0,24},{8,0},{16,8},{24,16},{1,25},{9,1},{17,9},{25,17},{2,26},{10... | collective-permute-start | bytes 786440 | tf_op jit(solution)/shard_map/cond/branch_0_fun/ppermute | solution.py:24
  107.9 6.5 %collective-permute-start.7 = (bf16[512,256]{1,0:T(8,128)(2,1)}, bf16[512,256]{1,0:T(8,128)(2,1)}, u32[]{:S(2)}, u32[]{:S(2)}) collective-permute-start(bf16[512,256]{1,0:T(8,128)(2,1)} %get-tuple-element.52), channel_id=1, source_target_pairs={{0,16},{8,24},{16,0},{24,8},{1,17},{9,25},{17,1},{25,9},{2,18},{10... | collective-permute-start | bytes 786440 | tf_op jit(solution)/shard_map/cond/branch_0_fun/ppermute | solution.py:24
  115.1 0.7 pad_maximum_fusion.5.bias_ref
  115.8 3.4 %collective-permute-done.5.refs_1_ = bf16[512,256]{1,0:T(8,128)(2,1)S(1)} collective-permute-done((bf16[512,256]{1,0:T(8,128)(2,1)}, bf16[512,256]{1,0:T(8,128)(2,1)S(1)}, u32[]{:S(2)}, u32[]{:S(2)}) %collective-permute-start.5) | collective-permute-done | bytes 262176 | tf_op jit(solution)/shard_map/cond/branch_0_fun/ppermute | solution.py:24
  119.2 3.3 %collective-permute-done.6.refs_2_ = bf16[512,256]{1,0:T(8,128)(2,1)S(1)} collective-permute-done((bf16[512,256]{1,0:T(8,128)(2,1)}, bf16[512,256]{1,0:T(8,128)(2,1)S(1)}, u32[]{:S(2)}, u32[]{:S(2)}) %collective-permute-start.6) | collective-permute-done | bytes 262176 | tf_op jit(solution)/shard_map/cond/branch_0_fun/ppermute | solution.py:24
  122.5 12.4 %collective-permute-done.7.refs_3_ = bf16[512,256]{1,0:T(8,128)(2,1)} collective-permute-done((bf16[512,256]{1,0:T(8,128)(2,1)}, bf16[512,256]{1,0:T(8,128)(2,1)}, u32[]{:S(2)}, u32[]{:S(2)}) %collective-permute-start.7) | collective-permute-done | bytes 262176 | tf_op jit(solution)/shard_map/cond/branch_0_fun/ppermute | solution.py:24
  134.9 2.6 %update.3 = (f32[256,512]{1,0:T(8,128)}, f32[256,512]{1,0:T(8,128)}, bf16[256,512]{1,0:T(8,128)(2,1)}) custom-call(f32[2]{0:T(128)} %pad_maximum_fusion.5.bias_ref, f32[256,512]{1,0:T(8,128)S(1)} %bitcast.93, f32[256,512]{1,0:T(8,128)S(1)} %bitcast.96, bf16[256,512]{1,0:T(8,128)(2,1)S(1)} %bitcast.74, f32[512,256]{1,0:T(8,128)} %get-tuple-element.49.refs_0_, ...), custom_call_target="tpu_custom_call" | custom-call | flops 3932160 | bytes 4456448 | tf_op jit(solution)/shard_map/cond/branch_0_fun/update/pallas_call | solution.py:196
  137.5 2.8 %collective-permute-start.8 = (bf16[256,512]{1,0:T(8,128)(2,1)}, bf16[256,512]{1,0:T(8,128)(2,1)S(1)}, u32[]{:S(2)}, u32[]{:S(2)}) collective-permute-start(bf16[256,512]{1,0:T(8,128)(2,1)} %get-tuple-element.53), channel_id=1, source_target_pairs={{480,0},{0,32},{32,64},{64,96},{96,128},{128,160},{160,192},{192,2... | collective-permute-start | bytes 786440 | tf_op jit(solution)/shard_map/cond/branch_0_fun/ppermute | solution.py:251
  140.3 0.8 fusion.2
  141.1 12.4 %collective-permute-done.8 = bf16[256,512]{1,0:T(8,128)(2,1)S(1)} collective-permute-done((bf16[256,512]{1,0:T(8,128)(2,1)}, bf16[256,512]{1,0:T(8,128)(2,1)S(1)}, u32[]{:S(2)}, u32[]{:S(2)}) %collective-permute-start.8) | collective-permute-done | bytes 262176 | tf_op jit(solution)/shard_map/cond/branch_0_fun/ppermute | solution.py:251
  153.5 1.7 %fusion = bf16[1,256,512]{2,1,0:T(8,128)(2,1)} fusion(bf16[256,512]{1,0:T(8,128)(2,1)S(1)} %collective-permute-done.8, bf16[256,512]{1,0:T(8,128)(2,1)} %get-tuple-element.53), kind=kLoop, calls=%fused_computation.11 | loop fusion | flops 655360 | bytes 786432 | tf_op jit(solution)/shard_map/cond/branch_0_fun/broadcast_in_dim | solution.py:253
  155.2 2.1 %finish_keys.3 = bf16[128,512]{1,0:T(8,128)(2,1)} custom-call(bf16[8,128,512]{2,1,0:T(8,128)(2,1)} %all-to-all-done.1.parts_ref, f32[128,128]{1,0:T(8,128)} %get-tuple-element.96.cosine_ref, f32[128,128]{1,0:T(8,128)} %get-tuple-element.95.sine_ref), custom_call_target="tpu_custom_call" | custom-call | flops 4194304 | bytes 1048576 | tf_op jit(solution)/shard_map/cond/branch_0_fun/finish_keys/pallas_call | solution.py:165
  (28 shorter events, 0.1 us)
Async XLA Ops:
  5.6 9.4 %copy-start = (bf16[1,256,512]{2,1,0:T(8,128)(2,1)S(1)}, bf16[1,256,512]{2,1,0:T(8,128)(2,1)}, u32[]{:S(2)}) copy-start(bf16[1,256,512]{2,1,0:T(8,128)(2,1)} %get-tuple-element.44) | copy-start | bytes 786436 | tf_op jit(solution)/shard_map/cond
  5.6 48.5 %copy-start.3 = (bf16[128,512]{1,0:T(8,128)(2,1)S(1)}, bf16[128,512]{1,0:T(8,128)(2,1)}, u32[]{:S(2)}) copy-start(bf16[128,512]{1,0:T(8,128)(2,1)} %get-tuple-element.48.own_ref) | copy-start | bytes 393220 | tf_op jit(solution)/shard_map/cond
  5.6 66.4 %all-to-all-start = ((bf16[8,128,1024]{2,1,0:T(8,128)(2,1)}), bf16[8,128,1024]{2,1,0:T(8,128)(2,1)S(1)}, u32[]{:S(2)}, u32[]{:S(2)}) async-start(bf16[8,128,1024]{2,1,0:T(8,128)(2,1)} %norm.3), calls=%async_computation | async-start | bytes 4194304 | tf_op jit(solution)/shard_map/cond/branch_0_fun/all_to_all | solution.py:224
  15.1 36.3 %collective-permute-start = (bf16[256,512]{1,0:T(8,128)(2,1)S(1)}, bf16[256,512]{1,0:T(8,128)(2,1)S(1)}, u32[]{:S(2)}, u32[]{:S(2)}) collective-permute-start(bf16[256,512]{1,0:T(8,128)(2,1)S(1)} %bitcast.72), channel_id=1, source_target_pairs={{0,16},{8,24},{16,0},{24,8},{1,17},{9,25},{17,1},{25,9},{2,18},{10... | collective-permute-start | bytes 786440 | tf_op jit(solution)/shard_map/cond/branch_0_fun/ppermute | solution.py:24
  51.3 20.7 %copy-start.18 = (bf16[256,512]{1,0:T(8,128)(2,1)}, bf16[256,512]{1,0:T(8,128)(2,1)S(1)}, u32[]{:S(2)}) copy-start(bf16[256,512]{1,0:T(8,128)(2,1)S(1)} %collective-permute-done.w2) | copy-start | bytes 786436 | tf_op jit(solution)/shard_map/cond
  52.2 19.8 %collective-permute-start.1 = (bf16[2,256,512]{2,1,0:T(8,128)(2,1)}, bf16[2,256,512]{2,1,0:T(8,128)(2,1)}, u32[]{:S(2)}, u32[]{:S(2)}) collective-permute-start(bf16[2,256,512]{2,1,0:T(8,128)(2,1)} %pad_maximum_fusion), channel_id=1, source_target_pairs={{8,0},{25,1},{16,8},{1,9},{24,16},{9,17},{0,24},{17,25},{10,2},{27... | collective-permute-start | bytes 1572872 | tf_op jit(solution)/shard_map/cond/branch_0_fun/ppermute | solution.py:33
  54.1 15.3 %collective-permute-start.2 = (bf16[128,512]{1,0:T(8,128)(2,1)S(1)}, bf16[128,512]{1,0:T(8,128)(2,1)S(1)}, u32[]{:S(2)}, u32[]{:S(2)}) collective-permute-start(bf16[128,512]{1,0:T(8,128)(2,1)S(1)} %copy-done.3), channel_id=1, source_target_pairs={{0,4},{4,0},{1,5},{5,1},{2,6},{6,2},{3,7},{7,3},{8,12},{12,8},{9,1... | collective-permute-start | bytes 393224 | tf_op jit(solution)/shard_map/cond/branch_0_fun/ppermute | solution.py:37
  69.4 16.9 %copy-start.15 = (bf16[128,512]{1,0:T(8,128)(2,1)}, bf16[128,512]{1,0:T(8,128)(2,1)S(1)}, u32[]{:S(2)}) copy-start(bf16[128,512]{1,0:T(8,128)(2,1)S(1)} %collective-permute-done.2.beside_ref) | copy-start | bytes 393220 | tf_op jit(solution)/shard_map/cond
  69.5 16.9 %collective-permute-start.3 = (bf16[2,128,512]{2,1,0:T(8,128)(2,1)S(1)}, bf16[2,128,512]{2,1,0:T(8,128)(2,1)S(1)}, u32[]{:S(2)}, u32[]{:S(2)}) collective-permute-start(bf16[2,128,512]{2,1,0:T(8,128)(2,1)S(1)} %pad_maximum_fusion.4), channel_id=1, source_target_pairs={{0,2},{2,0},{1,3},{3,1},{4,6},{6,4},{5,7},{7,5},{8,10},{10,8},{9,1... | collective-permute-start | bytes 786440 | tf_op jit(solution)/shard_map/cond/branch_0_fun/ppermute | solution.py:37
  72.0 1.3 copy-start.6
  77.4 77.8 %all-to-all-start.1 = ((bf16[8,128,512]{2,1,0:T(8,128)(2,1)}), bf16[8,128,512]{2,1,0:T(8,128)(2,1)}, u32[]{:S(2)}, u32[]{:S(2)}) async-start(bf16[8,128,512]{2,1,0:T(8,128)(2,1)} %forward.3), calls=%async_computation.1 | async-start | bytes 2097152 | tf_op jit(solution)/shard_map/cond/branch_0_fun/all_to_all | solution.py:243
  86.4 6.0 %copy-start.21 = (bf16[2,128,512]{2,1,0:T(8,128)(2,1)}, bf16[2,128,512]{2,1,0:T(8,128)(2,1)S(1)}, u32[]{:S(2)}) copy-start(bf16[2,128,512]{2,1,0:T(8,128)(2,1)S(1)} %collective-permute-done.3.two_ref) | copy-start | bytes 786436 | tf_op jit(solution)/shard_map/cond
  86.5 6.0 %collective-permute-start.4 = (bf16[4,128,512]{2,1,0:T(8,128)(2,1)S(1)}, bf16[4,128,512]{2,1,0:T(8,128)(2,1)}, u32[]{:S(2)}, u32[]{:S(2)}) collective-permute-start(bf16[4,128,512]{2,1,0:T(8,128)(2,1)S(1)} %pad_maximum_fusion.1), channel_id=1, source_target_pairs={{0,1},{1,0},{2,3},{3,2},{4,5},{5,4},{6,7},{7,6},{8,9},{9,8},{10,11... | collective-permute-start | bytes 1572872 | tf_op jit(solution)/shard_map/cond/branch_0_fun/ppermute | solution.py:37
  95.9 39.0 %copy-start.9 = (f32[1,256,512]{2,1,0:T(8,128)S(1)}, f32[1,256,512]{2,1,0:T(8,128)}, u32[]{:S(2)}) copy-start(f32[1,256,512]{2,1,0:T(8,128)} %get-tuple-element.46) | copy-start | bytes 1572868 | tf_op jit(solution)/shard_map/cond
  95.9 39.0 %copy-start.12 = (f32[1,256,512]{2,1,0:T(8,128)S(1)}, f32[1,256,512]{2,1,0:T(8,128)}, u32[]{:S(2)}) copy-start(f32[1,256,512]{2,1,0:T(8,128)} %get-tuple-element.47) | copy-start | bytes 1572868 | tf_op jit(solution)/shard_map/cond
  99.9 19.3 %collective-permute-start.5 = (bf16[512,256]{1,0:T(8,128)(2,1)}, bf16[512,256]{1,0:T(8,128)(2,1)S(1)}, u32[]{:S(2)}, u32[]{:S(2)}) collective-permute-start(bf16[512,256]{1,0:T(8,128)(2,1)} %get-tuple-element.50), channel_id=1, source_target_pairs={{0,8},{8,16},{16,24},{24,0},{1,9},{9,17},{17,25},{25,1},{2,10},{10... | collective-permute-start | bytes 786440 | tf_op jit(solution)/shard_map/cond/branch_0_fun/ppermute | solution.py:24
  104.7 17.7 %collective-permute-start.6 = (bf16[512,256]{1,0:T(8,128)(2,1)}, bf16[512,256]{1,0:T(8,128)(2,1)S(1)}, u32[]{:S(2)}, u32[]{:S(2)}) collective-permute-start(bf16[512,256]{1,0:T(8,128)(2,1)} %get-tuple-element.51), channel_id=1, source_target_pairs={{0,24},{8,0},{16,8},{24,16},{1,25},{9,1},{17,9},{25,17},{2,26},{10... | collective-permute-start | bytes 786440 | tf_op jit(solution)/shard_map/cond/branch_0_fun/ppermute | solution.py:24
  107.9 27.0 %collective-permute-start.7 = (bf16[512,256]{1,0:T(8,128)(2,1)}, bf16[512,256]{1,0:T(8,128)(2,1)}, u32[]{:S(2)}, u32[]{:S(2)}) collective-permute-start(bf16[512,256]{1,0:T(8,128)(2,1)} %get-tuple-element.52), channel_id=1, source_target_pairs={{0,16},{8,24},{16,0},{24,8},{1,17},{9,25},{17,1},{25,9},{2,18},{10... | collective-permute-start | bytes 786440 | tf_op jit(solution)/shard_map/cond/branch_0_fun/ppermute | solution.py:24
  119.2 15.7 %copy-start.24 = (bf16[512,256]{1,0:T(8,128)(2,1)}, bf16[512,256]{1,0:T(8,128)(2,1)S(1)}, u32[]{:S(2)}) copy-start(bf16[512,256]{1,0:T(8,128)(2,1)S(1)} %collective-permute-done.5.refs_1_) | copy-start | bytes 786436 | tf_op jit(solution)/shard_map/cond
  122.5 12.4 %copy-start.27 = (bf16[512,256]{1,0:T(8,128)(2,1)}, bf16[512,256]{1,0:T(8,128)(2,1)S(1)}, u32[]{:S(2)}) copy-start(bf16[512,256]{1,0:T(8,128)(2,1)S(1)} %collective-permute-done.6.refs_2_) | copy-start | bytes 786436 | tf_op jit(solution)/shard_map/cond
  137.5 16.0 %collective-permute-start.8 = (bf16[256,512]{1,0:T(8,128)(2,1)}, bf16[256,512]{1,0:T(8,128)(2,1)S(1)}, u32[]{:S(2)}, u32[]{:S(2)}) collective-permute-start(bf16[256,512]{1,0:T(8,128)(2,1)} %get-tuple-element.53), channel_id=1, source_target_pairs={{480,0},{0,32},{32,64},{64,96},{96,128},{128,160},{160,192},{192,2... | collective-permute-start | bytes 786440 | tf_op jit(solution)/shard_map/cond/branch_0_fun/ppermute | solution.py:251

commit v2 on v1

--- a/solution.py
+++ b/solution.py
@@ -16,7 +16,8 @@
 PLANE = ("h", "x", "c")
 EVERY = ("rep", "y", "h", "x", "c")
 DISTANCES = (1, 2, 4)
-SENDS = (1, 3, 2)
+CHUNKS = ((2, 1), (3, 0))
+SENDS = (2, 1, 3)
 BF16, F32 = jnp.bfloat16, jnp.float32
 
 
@@ -52,31 +53,54 @@
     return values * cosine + pltpu.roll(values, HEAD // 2, 1) * sine
 
 
-def norm_kernel(y_ref, rows_ref, gain_ref, out_ref):
-    values = rows_ref[...].astype(F32)
-    inverse = lax.rsqrt(jnp.mean(values * values, axis=-1, keepdims=True) + 1e-05)
+def put_blocks(y, order, rows_ref, inverse, gain_ref, out_ref):
     feat = rows_ref.shape[1] // (NY * NP)
-    for k in range(NY):
-        block = lax.rem(y_ref[0] + k, NY)
+    for place, k in enumerate(order):
+        block = lax.rem(y + k, NY)
         for p in range(NP):
             start = pl.multiple_of((block * NP + p) * feat, 128)
             part = rows_ref[:, pl.ds(start, feat)].astype(F32)
             normed = part * inverse * gain_ref[:, pl.ds(start, feat)]
-            out_ref[p, :, k * feat : (k + 1) * feat] = normed.astype(BF16)
-
-
-def norm(y, hidden, gain):
+            out_ref[p, :, place * feat : (place + 1) * feat] = normed.astype(BF16)
+
+
+def norm_first_kernel(y_ref, rows_ref, gain_ref, out_ref, inverse_ref):
+    values = rows_ref[...].astype(F32)
+    inverse = lax.rsqrt(jnp.mean(values * values, axis=-1, keepdims=True) + 1e-05)
+    inverse_ref[...] = jnp.broadcast_to(inverse, inverse_ref.shape)
+    put_blocks(y_ref[0], CHUNKS[0], rows_ref, inverse, gain_ref, out_ref)
+
+
+def norm_second_kernel(y_ref, rows_ref, gain_ref, inverse_ref, out_ref):
+    put_blocks(y_ref[0], CHUNKS[1], rows_ref, inverse_ref[:, :1], gain_ref, out_ref)
+
+
+def norm(y, hidden, gain, inverse=None):
     rows, width = hidden.shape
     step = 32
-    return pl.pallas_call(
-        norm_kernel,
-        grid=(rows // step,),
-        in_specs=[SMEM, pl.BlockSpec((step, width), lambda i: (i, 0)), pl.BlockSpec((1, width), lambda i: (0, 0))],
-        out_specs=pl.BlockSpec((NP, step, width // NP), lambda i: (0, i, 0)),
-        out_shape=jax.ShapeDtypeStruct((NP, rows, width // NP), BF16),
-        cost_estimate=cost(6 * rows * width, 4 * rows * width),
-        name="norm",
-    )(y, hidden, gain)
+    span = 2 * (width // (NY * NP))
+    in_specs = [SMEM, pl.BlockSpec((step, width), lambda i: (i, 0)), pl.BlockSpec((1, width), lambda i: (0, 0))]
+    out_spec = pl.BlockSpec((NP, step, span), lambda i: (0, i, 0))
+    out_shape = jax.ShapeDtypeStruct((NP, rows, span), BF16)
+    stat_spec = pl.BlockSpec((step, 128), lambda i: (i, 0))
+    shared = dict(grid=(rows // step,), cost_estimate=cost(4 * rows * width, 3 * rows * width))
+    if inverse is None:
+        return pl.pallas_call(
+            norm_first_kernel,
+            in_specs=in_specs,
+            out_specs=[out_spec, stat_spec],
+            out_shape=[out_shape, jax.ShapeDtypeStruct((rows, 128), F32)],
+            name="norm_first",
+            **shared,
+        )(y, hidden, gain)
+    return pl.pallas_call(
+        norm_second_kernel,
+        in_specs=in_specs + [stat_spec],
+        out_specs=out_spec,
+        out_shape=out_shape,
+        name="norm_second",
+        **shared,
+    )(y, hidden, gain, inverse)
 
 
 def turn_back_kernel(at_ref, own_ref, beside_ref, two_ref, four_ref, cosine_ref, sine_ref, out_ref):
@@ -105,51 +129,52 @@
 
 def grads_kernel(tokens_ref, dpre_ref, *outs):
     feat = outs[0].shape[1]
-    for k, out in enumerate(outs):
-        block = tokens_ref[:, k * feat : (k + 1) * feat]
+    for place, out in enumerate(outs):
+        block = tokens_ref[:, place * feat : (place + 1) * feat]
         out[...] = jnp.dot(dpre_ref[...], block, preferred_element_type=F32).astype(out.dtype)
 
 
-def grads(tokens, dpre):
+def grads(tokens, dpre, order):
     count, width = tokens.shape
     kvw = dpre.shape[0]
-    feat = width // NY
+    feat = width // len(order)
     return pl.pallas_call(
         grads_kernel,
         in_specs=vmem(2),
-        out_specs=vmem(NY),
-        out_shape=[jax.ShapeDtypeStruct((kvw, feat), BF16 if k else F32) for k in range(NY)],
+        out_specs=vmem(len(order)),
+        out_shape=[jax.ShapeDtypeStruct((kvw, feat), BF16 if k else F32) for k in order],
         cost_estimate=cost(2 * count * width * kvw, 2 * count * width + 3 * width * kvw),
         name="grads",
     )(tokens, dpre)
 
 
-def forward_kernel(core_ref, tokens_ref, w0, w2, pair_ref, out_ref):
+def forward_kernel(core_ref, a_ref, b_ref, w0, w2, pair_ref, out_ref):
     feat = w0.shape[0]
     rows = out_ref.shape[1]
-    here = pl.multiple_of((1 + 2 * core_ref[0]) * feat, 128)
-    there = pl.multiple_of((3 - 2 * core_ref[0]) * feat, 128)
+    core = core_ref[0]
+    w1 = pair_ref[core]
+    w3 = pair_ref[1 - core]
+    held = {0: w0[...], 1: w1, 2: w2[...], 3: w3}
     for p in range(NP):
         mine = slice(p * rows, (p + 1) * rows)
-
-        def term(start, weight):
-            return jnp.dot(tokens_ref[mine, pl.ds(start, feat)], weight, preferred_element_type=F32)
-
-        total = term(0, w0[...]) + term(2 * feat, w2[...]) + term(here, pair_ref[0]) + term(there, pair_ref[1])
+        total = jnp.zeros(out_ref.shape[1:], F32)
+        for ref, order in zip((a_ref, b_ref), CHUNKS):
+            for place, k in enumerate(order):
+                total += jnp.dot(ref[mine, place * feat : (place + 1) * feat], held[k], preferred_element_type=F32)
         out_ref[p] = total.astype(out_ref.dtype)
 
 
-def forward(core, tokens, weights):
-    count, width = tokens.shape
-    kvw = weights[0].shape[1]
+def forward(core, chunks, weights):
+    count, kvw = chunks[0].shape[0], weights[0].shape[1]
+    flops = 2 * count * kvw * sum(chunk.shape[1] for chunk in chunks)
     return pl.pallas_call(
         forward_kernel,
-        in_specs=[SMEM] + vmem(1 + len(weights)),
+        in_specs=[SMEM] + vmem(len(chunks) + len(weights)),
         out_specs=pl.BlockSpec(memory_space=pltpu.VMEM),
         out_shape=jax.ShapeDtypeStruct((NP, count // NP, kvw), BF16),
-        cost_estimate=cost(2 * count * width * kvw, 5 << 20),
+        cost_estimate=cost(flops, 5 << 20),
         name="forward",
-    )(core, tokens, *weights)
+    )(core, *chunks, *weights)
 
 
 def keys_kernel(scale, parts_ref, cosine_ref, sine_ref, out_ref):
@@ -219,9 +244,12 @@
     y, h, x, c = [lax.axis_index(axis).astype(jnp.int32) for axis in GROUP]
 
     beside = across(dkeys, "h")
-    tokens = norm(y.reshape(1), hidden, gain.reshape(1, -1))
+    at_y, gain = y.reshape(1), gain.reshape(1, -1)
+    first, inverse = norm(at_y, hidden, gain)
     two = across(jnp.stack([dkeys, beside]), "x")
-    tokens = lax.all_to_all(tokens, PLANE, 0, 0, tiled=True).reshape(NP * rows, -1)
+    first = lax.all_to_all(first, PLANE, 0, 0, tiled=True).reshape(NP * rows, -1)
+    later = norm(at_y, hidden, gain, inverse)
+    later = lax.all_to_all(later, PLANE, 0, 0, tiled=True).reshape(NP * rows, -1)
     four = across(jnp.concatenate([jnp.stack([dkeys, beside]), two]), "c")
     cosine, sine = rotation(y * NP * rows + jnp.arange(NP * rows))
     at = jnp.stack(
@@ -234,12 +262,14 @@
     w2 = shifted(weight, 2)
     pair = toward(jnp.stack([weight, w2]))
 
-    blocks = grads(tokens, dpre)
+    blocks = {}
+    for chunk, order in zip((first, later), CHUNKS):
+        blocks.update(zip(order, grads(chunk, dpre, order)))
     arrived = [blocks[0]]
     for k in SENDS:
         arrived.append(shifted(blocks[k], k))
 
-    parts = forward(c.reshape(1), tokens, (weight, w2, pair))
+    parts = forward(c.reshape(1), (first, later), (weight, w2, pair))
     parts = lax.all_to_all(parts, PLANE, 0, 0, tiled=True)
     keys = finish_keys(parts, cosine, sine, scale)
 

time: 158 us -> 164 us (1.038)
  waiting for transfers between devices: 77.4 us -> 70.4 us
  starting transfers between devices: 47.8 us -> 54.6 us
  Pallas kernels: 20.6 us -> 25.7 us
    ppermute x4, waiting for transfers between devices: 52.1 us -> 34.4 us  [shifted(): lax.ppermute(block, 'y', [(i, (i + distance) % NY) for i in range(NY)])]
    all_to_all x1 -> x2, waiting for transfers between devices: 0.01 us -> 9.85 us  [the longest x1 9.84 us: one_distance(): lax.all_to_all(first, PLANE, 0, 0, tiled=True).reshape(NP * rows, -1)]
    all_to_all x1 -> x2, starting transfers between devices: 9.41 us -> 15.6 us  [the longest x1 9.23 us: one_distance(): lax.all_to_all(first, PLANE, 0, 0, tiled=True).reshape(NP * rows, -1)]
    pallas_call x3 -> x5, Pallas kernels: 12.4 us -> 17.5 us  [the longest x2 6.25 us: grads(): pl.pallas_call(grads_kernel, in_specs=vmem(2), out_specs=vmem(len(order))...]
  transfers between devices with their start and end apart: 11 -> 12, of which waited for: 6 -> 5; matrix products, arithmetic and copies ran while one was open for 5% -> 5% of each run, Pallas kernels for 9% -> 12%
where the time goes in v2:
time: 164 us; the launch traced here: 163 us
  waiting for transfers between devices  70.4 us (43%)
  starting transfers between devices  54.6 us (33%)
  Pallas kernels  25.7 us (16%)
  other arithmetic  7.31 us (4%)
  local copies, waits for them, and re-layouts  2.31 us (1%)
    ppermute x4, waiting for transfers between devices, shifted(): lax.ppermute(block, 'y', [(i, (i + distance) % NY) for i in range(NY)])  34.4 us
    ppermute x4, starting transfers between devices, shifted(): lax.ppermute(block, 'y', [(i, (i + distance) % NY) for i in range(NY)])  17.7 us
    ppermute x1, waiting for transfers between devices, one_distance(): lax.ppermute(local, 'rep', [((i - distance) % groups, i) for i in range(g...  13.2 us
    ppermute x3, waiting for transfers between devices, across(): return lax.ppermute(block, axis, [(0, 1), (1, 0)])  12.9 us
    all_to_all x1, waiting for transfers between devices, one_distance(): lax.all_to_all(first, PLANE, 0, 0, tiled=True).reshape(NP * rows, -1)  9.84 us
    all_to_all x1, starting transfers between devices, one_distance(): lax.all_to_all(first, PLANE, 0, 0, tiled=True).reshape(NP * rows, -1)  9.23 us
    all_to_all x1, starting transfers between devices, one_distance(): parts = lax.all_to_all(parts, PLANE, 0, 0, tiled=True)  9.02 us
    ppermute x3, starting transfers between devices, across(): return lax.ppermute(block, axis, [(0, 1), (1, 0)])  6.98 us
  transfers between devices with their start and end apart: 12, of which 5 were waited for; matrix products, arithmetic and copies ran while one was open for 5% of the time, Pallas kernels for 12%

profile of v2, /device:TPU:12, one launch (start us, length us, event | category | flops | bytes accessed | tf_op | source)
XLA Modules:
  0.0 162.7 jit_solution(5232032632476938216)
XLA Ops:
  1.3 161.4 %conditional.1 = (bf16[128,512]{1,0:T(8,128)(2,1)}, bf16[1,256,512]{2,1,0:T(8,128)(2,1)}, f32[1,256,512]{2,1,0:T(8,128)}, f32[1,256,512]{2,1,0:T(8,128)}) conditional(s32[]{:T(128)} %clamp.3, (f32[8192]{0:T(1024)}, bf16[128,8192]{1,0:T(8,128)(2,1)}, bf16[1,256,512]{2,1,0:T(8,128)(2,1)}, s32[]{:T(128)}, f32[1,256,512]{2,1,0:T(8,128)}, ...), branch_computations={%region_0.1_spmd, %region_1.2_spmd, %region_2.3_spmd} | conditional | flops 2170193920 | bytes 78653304 | solution.py:293
  1.3 4.2 %norm_first.3 = (bf16[8,128,512]{2,1,0:T(8,128)(2,1)}, f32[128,128]{1,0:T(8,128)}) custom-call(s32[1]{0:T(128)} %bitcast.1.y_ref, bf16[128,8192]{1,0:T(8,128)(2,1)} %get-tuple-element.42.rows_ref, f32[1,8192]{1,0:T(1,128)} %bitcast.108), custom_call_target="tpu_custom_call" | custom-call | flops 4194304 | bytes 3145728 | tf_op jit(solution)/shard_map/cond/branch_0_fun/norm_first/pallas_call | solution.py:88
  5.5 9.2 %all-to-all-start = ((bf16[8,128,512]{2,1,0:T(8,128)(2,1)}), bf16[8,128,512]{2,1,0:T(8,128)(2,1)S(1)}, u32[]{:S(2)}, u32[]{:S(2)}) async-start(bf16[8,128,512]{2,1,0:T(8,128)(2,1)} %get-tuple-element.44), calls=%async_computation | async-start | bytes 2097152 | tf_op jit(solution)/shard_map/cond/branch_0_fun/all_to_all | solution.py:250
  14.8 3.1 %norm_second.3 = bf16[8,128,512]{2,1,0:T(8,128)(2,1)} custom-call(s32[1]{0:T(128)} %bitcast.1.y_ref, bf16[128,8192]{1,0:T(8,128)(2,1)S(1)} %copy-done, f32[1,8192]{1,0:T(1,128)S(1)} %bitcast.109, f32[128,128]{1,0:T(8,128)} %get-tuple-element.45.inverse_ref), custom_call_target="tpu_custom_call" | custom-call | flops 4194304 | bytes 3145728 | tf_op jit(solution)/shard_map/cond/branch_0_fun/norm_second/pallas_call | solution.py:96
  17.9 9.8 %all-to-all-done = bf16[8,128,512]{2,1,0:T(8,128)(2,1)S(1)} async-done(((bf16[8,128,512]{2,1,0:T(8,128)(2,1)}), bf16[8,128,512]{2,1,0:T(8,128)(2,1)S(1)}, u32[]{:S(2)}, u32[]{:S(2)}) %all-to-all-start) | async-done | bytes 1048608 | tf_op jit(solution)/shard_map/cond/branch_0_fun/all_to_all | solution.py:250
  27.7 6.4 %all-to-all-start.1 = ((bf16[8,128,512]{2,1,0:T(8,128)(2,1)}), bf16[8,128,512]{2,1,0:T(8,128)(2,1)S(1)}, u32[]{:S(2)}, u32[]{:S(2)}) async-start(bf16[8,128,512]{2,1,0:T(8,128)(2,1)} %norm_second.3), calls=%async_computation.1 | async-start | bytes 2097152 | tf_op jit(solution)/shard_map/cond/branch_0_fun/all_to_all | solution.py:252
  34.1 3.3 %collective-permute-start = (bf16[256,512]{1,0:T(8,128)(2,1)S(1)}, bf16[256,512]{1,0:T(8,128)(2,1)S(1)}, u32[]{:S(2)}, u32[]{:S(2)}) collective-permute-start(bf16[256,512]{1,0:T(8,128)(2,1)S(1)} %bitcast.75), channel_id=1, source_target_pairs={{0,16},{8,24},{16,0},{24,8},{1,17},{9,25},{17,1},{25,9},{2,18},{10... | collective-permute-start | bytes 786440 | tf_op jit(solution)/shard_map/cond/branch_0_fun/ppermute | solution.py:25
  37.5 21.8 %collective-permute-done.w2 = bf16[256,512]{1,0:T(8,128)(2,1)S(1)} collective-permute-done((bf16[256,512]{1,0:T(8,128)(2,1)S(1)}, bf16[256,512]{1,0:T(8,128)(2,1)S(1)}, u32[]{:S(2)}, u32[]{:S(2)}) %collective-permute-start) | collective-permute-done | bytes 262176 | tf_op jit(solution)/shard_map/cond/branch_0_fun/ppermute | solution.py:25
  59.3 0.9 pad_maximum_fusion
  60.1 1.9 %collective-permute-start.1 = (bf16[2,256,512]{2,1,0:T(8,128)(2,1)}, bf16[2,256,512]{2,1,0:T(8,128)(2,1)}, u32[]{:S(2)}, u32[]{:S(2)}) collective-permute-start(bf16[2,256,512]{2,1,0:T(8,128)(2,1)} %pad_maximum_fusion), channel_id=1, source_target_pairs={{8,0},{25,1},{16,8},{1,9},{24,16},{9,17},{0,24},{17,25},{10,2},{27... | collective-permute-start | bytes 1572872 | tf_op jit(solution)/shard_map/cond/branch_0_fun/ppermute | solution.py:34
  62.1 2.4 %collective-permute-start.2 = (bf16[128,512]{1,0:T(8,128)(2,1)S(1)}, bf16[128,512]{1,0:T(8,128)(2,1)S(1)}, u32[]{:S(2)}, u32[]{:S(2)}) collective-permute-start(bf16[128,512]{1,0:T(8,128)(2,1)S(1)} %copy-done.6), channel_id=1, source_target_pairs={{0,4},{4,0},{1,5},{5,1},{2,6},{6,2},{3,7},{7,3},{8,12},{12,8},{9,1... | collective-permute-start | bytes 393224 | tf_op jit(solution)/shard_map/cond/branch_0_fun/ppermute | solution.py:38
  64.5 12.8 %collective-permute-done.2.beside_ref = bf16[128,512]{1,0:T(8,128)(2,1)S(1)} collective-permute-done((bf16[128,512]{1,0:T(8,128)(2,1)S(1)}, bf16[128,512]{1,0:T(8,128)(2,1)S(1)}, u32[]{:S(2)}, u32[]{:S(2)}) %collective-permute-start.2) | collective-permute-done | bytes 131104 | tf_op jit(solution)/shard_map/cond/branch_0_fun/ppermute | solution.py:38
  77.4 2.5 %collective-permute-start.3 = (bf16[2,128,512]{2,1,0:T(8,128)(2,1)S(1)}, bf16[2,128,512]{2,1,0:T(8,128)(2,1)S(1)}, u32[]{:S(2)}, u32[]{:S(2)}) collective-permute-start(bf16[2,128,512]{2,1,0:T(8,128)(2,1)S(1)} %pad_maximum_fusion.4), channel_id=1, source_target_pairs={{0,2},{2,0},{1,3},{3,1},{4,6},{6,4},{5,7},{7,5},{8,10},{10,8},{9,1... | collective-permute-start | bytes 786440 | tf_op jit(solution)/shard_map/cond/branch_0_fun/ppermute | solution.py:38
  80.0 1.0 copy-done.12
  80.9 4.0 %forward.3 = bf16[8,128,512]{2,1,0:T(8,128)(2,1)} custom-call(s32[1]{0:T(128)} %bitcast.core_ref, bf16[1024,512]{1,0:T(8,128)(2,1)} %bitcast.90, bf16[1024,512]{1,0:T(8,128)(2,1)} %bitcast.96, bf16[256,512]{1,0:T(8,128)(2,1)S(1)} %bitcast.76, bf16[256,512]{1,0:T(8,128)(2,1)} %copy-done.27, bf16[2,256,512]{2,1,0:T(8,128)(2,1)} %collective-permute-done.1.pair_ref), custom_call_target="tpu_custom_call" | custom-call | flops 1073741824 | bytes 5242880 | tf_op jit(solution)/shard_map/cond/branch_0_fun/forward/pallas_call | solution.py:170
  84.9 9.0 %all-to-all-start.2 = ((bf16[8,128,512]{2,1,0:T(8,128)(2,1)}), bf16[8,128,512]{2,1,0:T(8,128)(2,1)}, u32[]{:S(2)}, u32[]{:S(2)}) async-start(bf16[8,128,512]{2,1,0:T(8,128)(2,1)} %forward.3), calls=%async_computation.2 | async-start | bytes 2097152 | tf_op jit(solution)/shard_map/cond/branch_0_fun/all_to_all | solution.py:273
  94.0 2.0 %collective-permute-start.4 = (bf16[4,128,512]{2,1,0:T(8,128)(2,1)S(1)}, bf16[4,128,512]{2,1,0:T(8,128)(2,1)}, u32[]{:S(2)}, u32[]{:S(2)}) collective-permute-start(bf16[4,128,512]{2,1,0:T(8,128)(2,1)S(1)} %pad_maximum_fusion.1), channel_id=1, source_target_pairs={{0,1},{1,0},{2,3},{3,2},{4,5},{5,4},{6,7},{7,6},{8,9},{9,8},{10,11... | collective-permute-start | bytes 1572872 | tf_op jit(solution)/shard_map/cond/branch_0_fun/ppermute | solution.py:38
  96.7 1.9 %multiply_sine_fusion = (f32[1024,64]{1,0:T(8,128)S(1)}, f32[1024,64]{1,0:T(8,128)S(1)}, f32[1024,64]{1,0:T(8,128)S(1)}) fusion(f32[64]{0:T(128)S(1)} %multiply_exponential_fusion, f32[1024]{0:T(1024)S(1)} %add_convert_fusion), kind=kLoop, calls=%fused_computation | loop fusion | flops 131072 | bytes 790784 | tf_op jit(solution)/shard_map/cond/branch_0_fun/sin | solution.py:236
  98.6 1.3 pad_maximum_fusion.2
  99.9 3.5 %turn_back.3.dpre_ref = bf16[512,1024]{1,0:T(8,128)(2,1)} custom-call(s32[8]{0:T(128)} %stack.121.at_ref, bf16[128,512]{1,0:T(8,128)(2,1)S(1)} %copy-done.6, bf16[128,512]{1,0:T(8,128)(2,1)} %copy-done.24, bf16[2,128,512]{2,1,0:T(8,128)(2,1)} %copy-done.30, bf16[4,128,512]{2,1,0:T(8,128)(2,1)} %collective-permute-done.4.four_ref, ...), custom_call_target="tpu_custom_call" | custom-call | flops 4194304 | bytes 3145728 | tf_op jit(solution)/shard_map/cond/branch_0_fun/turn_back/pallas_call | solution.py:120
  103.4 3.1 %grads.7 = (bf16[512,256]{1,0:T(8,128)(2,1)}, bf16[512,256]{1,0:T(8,128)(2,1)}) custom-call(bf16[1024,512]{1,0:T(8,128)(2,1)} %bitcast.91, bf16[512,1024]{1,0:T(8,128)(2,1)} %turn_back.3.dpre_ref), custom_call_target="tpu_custom_call" | custom-call | flops 536870912 | bytes 1835008 | tf_op jit(solution)/shard_map/cond/branch_0_fun/grads/pallas_call | solution.py:141
  106.5 6.4 %collective-permute-start.5 = (bf16[512,256]{1,0:T(8,128)(2,1)}, bf16[512,256]{1,0:T(8,128)(2,1)S(1)}, u32[]{:S(2)}, u32[]{:S(2)}) collective-permute-start(bf16[512,256]{1,0:T(8,128)(2,1)} %get-tuple-element.52), channel_id=1, source_target_pairs={{0,16},{8,24},{16,0},{24,8},{1,17},{9,25},{17,1},{25,9},{2,18},{10... | collective-permute-start | bytes 786440 | tf_op jit(solution)/shard_map/cond/branch_0_fun/ppermute | solution.py:25
  112.9 3.1 %grads.6 = (bf16[512,256]{1,0:T(8,128)(2,1)}, f32[512,256]{1,0:T(8,128)}) custom-call(bf16[1024,512]{1,0:T(8,128)(2,1)} %bitcast.97, bf16[512,1024]{1,0:T(8,128)(2,1)} %turn_back.3.dpre_ref), custom_call_target="tpu_custom_call" | custom-call | flops 536870912 | bytes 1835008 | tf_op jit(solution)/shard_map/cond/branch_0_fun/grads/pallas_call | solution.py:141
  116.1 3.4 %collective-permute-start.6 = (bf16[512,256]{1,0:T(8,128)(2,1)}, bf16[512,256]{1,0:T(8,128)(2,1)S(1)}, u32[]{:S(2)}, u32[]{:S(2)}) collective-permute-start(bf16[512,256]{1,0:T(8,128)(2,1)} %get-tuple-element.53), channel_id=1, source_target_pairs={{0,8},{8,16},{16,24},{24,0},{1,9},{9,17},{17,25},{25,1},{2,10},{10... | collective-permute-start | bytes 786440 | tf_op jit(solution)/shard_map/cond/branch_0_fun/ppermute | solution.py:25
  119.4 4.6 %collective-permute-start.7 = (bf16[512,256]{1,0:T(8,128)(2,1)}, bf16[512,256]{1,0:T(8,128)(2,1)}, u32[]{:S(2)}, u32[]{:S(2)}) collective-permute-start(bf16[512,256]{1,0:T(8,128)(2,1)} %get-tuple-element.54), channel_id=1, source_target_pairs={{0,24},{8,0},{16,8},{24,16},{1,25},{9,1},{17,9},{25,17},{2,26},{10... | collective-permute-start | bytes 786440 | tf_op jit(solution)/shard_map/cond/branch_0_fun/ppermute | solution.py:25
  125.4 12.6 %collective-permute-done.6.refs_2_ = bf16[512,256]{1,0:T(8,128)(2,1)S(1)} collective-permute-done((bf16[512,256]{1,0:T(8,128)(2,1)}, bf16[512,256]{1,0:T(8,128)(2,1)S(1)}, u32[]{:S(2)}, u32[]{:S(2)}) %collective-permute-start.6) | collective-permute-done | bytes 262176 | tf_op jit(solution)/shard_map/cond/branch_0_fun/ppermute | solution.py:25
  138.8 2.6 %update.3 = (f32[256,512]{1,0:T(8,128)}, f32[256,512]{1,0:T(8,128)}, bf16[256,512]{1,0:T(8,128)(2,1)}) custom-call(f32[2]{0:T(128)} %pad_maximum_fusion.5.bias_ref, f32[256,512]{1,0:T(8,128)S(1)} %bitcast.102, f32[256,512]{1,0:T(8,128)S(1)} %bitcast.105, bf16[256,512]{1,0:T(8,128)(2,1)S(1)} %bitcast.77, f32[512,256]{1,0:T(8,128)} %get-tuple-element.51.refs_0_, ...), custom_call_target="tpu_custom_call" | custom-call | flops 3932160 | bytes 4456448 | tf_op jit(solution)/shard_map/cond/branch_0_fun/update/pallas_call | solution.py:221
  141.3 3.4 %collective-permute-start.8 = (bf16[256,512]{1,0:T(8,128)(2,1)}, bf16[256,512]{1,0:T(8,128)(2,1)S(1)}, u32[]{:S(2)}, u32[]{:S(2)}) collective-permute-start(bf16[256,512]{1,0:T(8,128)(2,1)} %get-tuple-element.55), channel_id=1, source_target_pairs={{480,0},{0,32},{32,64},{64,96},{96,128},{128,160},{160,192},{192,2... | collective-permute-start | bytes 786440 | tf_op jit(solution)/shard_map/cond/branch_0_fun/ppermute | solution.py:281
  144.8 0.8 fusion.2
  145.5 13.2 %collective-permute-done.8 = bf16[256,512]{1,0:T(8,128)(2,1)S(1)} collective-permute-done((bf16[256,512]{1,0:T(8,128)(2,1)}, bf16[256,512]{1,0:T(8,128)(2,1)S(1)}, u32[]{:S(2)}, u32[]{:S(2)}) %collective-permute-start.8) | collective-permute-done | bytes 262176 | tf_op jit(solution)/shard_map/cond/branch_0_fun/ppermute | solution.py:281
  158.8 1.7 %fusion = bf16[1,256,512]{2,1,0:T(8,128)(2,1)} fusion(bf16[256,512]{1,0:T(8,128)(2,1)S(1)} %collective-permute-done.8, bf16[256,512]{1,0:T(8,128)(2,1)} %get-tuple-element.55), kind=kLoop, calls=%fused_computation.11 | loop fusion | flops 655360 | bytes 786432 | tf_op jit(solution)/shard_map/cond/branch_0_fun/broadcast_in_dim | solution.py:283
  160.5 2.1 %finish_keys.3 = bf16[128,512]{1,0:T(8,128)(2,1)} custom-call(bf16[8,128,512]{2,1,0:T(8,128)(2,1)} %all-to-all-done.2.parts_ref, f32[128,128]{1,0:T(8,128)} %get-tuple-element.102.cosine_ref, f32[128,128]{1,0:T(8,128)} %get-tuple-element.101.sine_ref), custom_call_target="tpu_custom_call" | custom-call | flops 4194304 | bytes 1048576 | tf_op jit(solution)/shard_map/cond/branch_0_fun/finish_keys/pallas_call | solution.py:190
  (38 shorter events, 2.1 us)
Async XLA Ops:
  1.3 13.4 %copy-start = (bf16[128,8192]{1,0:T(8,128)(2,1)S(1)}, bf16[128,8192]{1,0:T(8,128)(2,1)}, u32[]{:S(2)}) copy-start(bf16[128,8192]{1,0:T(8,128)(2,1)} %get-tuple-element.42.rows_ref) | copy-start | bytes 6291460 | tf_op jit(solution)/shard_map/cond
  1.3 13.4 %copy-start.21 = (f32[8192]{0:T(1024)S(1)}, f32[8192]{0:T(1024)}, u32[]{:S(2)}) copy-start(f32[8192]{0:T(1024)} %get-tuple-element.43) | copy-start | bytes 98308 | tf_op jit(solution)/shard_map/cond
  5.5 22.2 %all-to-all-start = ((bf16[8,128,512]{2,1,0:T(8,128)(2,1)}), bf16[8,128,512]{2,1,0:T(8,128)(2,1)S(1)}, u32[]{:S(2)}, u32[]{:S(2)}) async-start(bf16[8,128,512]{2,1,0:T(8,128)(2,1)} %get-tuple-element.44), calls=%async_computation | async-start | bytes 2097152 | tf_op jit(solution)/shard_map/cond/branch_0_fun/all_to_all | solution.py:250
  14.7 19.4 %copy-start.3 = (bf16[1,256,512]{2,1,0:T(8,128)(2,1)S(1)}, bf16[1,256,512]{2,1,0:T(8,128)(2,1)}, u32[]{:S(2)}) copy-start(bf16[1,256,512]{2,1,0:T(8,128)(2,1)} %get-tuple-element.46) | copy-start | bytes 786436 | tf_op jit(solution)/shard_map/cond
  17.9 44.2 %copy-start.6 = (bf16[128,512]{1,0:T(8,128)(2,1)S(1)}, bf16[128,512]{1,0:T(8,128)(2,1)}, u32[]{:S(2)}) copy-start(bf16[128,512]{1,0:T(8,128)(2,1)} %get-tuple-element.50.own_ref) | copy-start | bytes 393220 | tf_op jit(solution)/shard_map/cond
  27.7 52.2 %copy-start.9 = (bf16[8,128,512]{2,1,0:T(8,128)(2,1)}, bf16[8,128,512]{2,1,0:T(8,128)(2,1)S(1)}, u32[]{:S(2)}) copy-start(bf16[8,128,512]{2,1,0:T(8,128)(2,1)S(1)} %all-to-all-done) | copy-start | bytes 3145732 | tf_op jit(solution)/shard_map/cond
  27.7 52.2 %all-to-all-start.1 = ((bf16[8,128,512]{2,1,0:T(8,128)(2,1)}), bf16[8,128,512]{2,1,0:T(8,128)(2,1)S(1)}, u32[]{:S(2)}, u32[]{:S(2)}) async-start(bf16[8,128,512]{2,1,0:T(8,128)(2,1)} %norm_second.3), calls=%async_computation.1 | async-start | bytes 2097152 | tf_op jit(solution)/shard_map/cond/branch_0_fun/all_to_all | solution.py:252
  34.1 25.1 %collective-permute-start = (bf16[256,512]{1,0:T(8,128)(2,1)S(1)}, bf16[256,512]{1,0:T(8,128)(2,1)S(1)}, u32[]{:S(2)}, u32[]{:S(2)}) collective-permute-start(bf16[256,512]{1,0:T(8,128)(2,1)S(1)} %bitcast.75), channel_id=1, source_target_pairs={{0,16},{8,24},{16,0},{24,8},{1,17},{9,25},{17,1},{25,9},{2,18},{10... | collective-permute-start | bytes 786440 | tf_op jit(solution)/shard_map/cond/branch_0_fun/ppermute | solution.py:25
  59.3 20.7 %copy-start.27 = (bf16[256,512]{1,0:T(8,128)(2,1)}, bf16[256,512]{1,0:T(8,128)(2,1)S(1)}, u32[]{:S(2)}) copy-start(bf16[256,512]{1,0:T(8,128)(2,1)S(1)} %collective-permute-done.w2) | copy-start | bytes 786436 | tf_op jit(solution)/shard_map/cond
  60.1 19.8 %collective-permute-start.1 = (bf16[2,256,512]{2,1,0:T(8,128)(2,1)}, bf16[2,256,512]{2,1,0:T(8,128)(2,1)}, u32[]{:S(2)}, u32[]{:S(2)}) collective-permute-start(bf16[2,256,512]{2,1,0:T(8,128)(2,1)} %pad_maximum_fusion), channel_id=1, source_target_pairs={{8,0},{25,1},{16,8},{1,9},{24,16},{9,17},{0,24},{17,25},{10,2},{27... | collective-permute-start | bytes 1572872 | tf_op jit(solution)/shard_map/cond/branch_0_fun/ppermute | solution.py:34
  62.1 15.3 %collective-permute-start.2 = (bf16[128,512]{1,0:T(8,128)(2,1)S(1)}, bf16[128,512]{1,0:T(8,128)(2,1)S(1)}, u32[]{:S(2)}, u32[]{:S(2)}) collective-permute-start(bf16[128,512]{1,0:T(8,128)(2,1)S(1)} %copy-done.6), channel_id=1, source_target_pairs={{0,4},{4,0},{1,5},{5,1},{2,6},{6,2},{3,7},{7,3},{8,12},{12,8},{9,1... | collective-permute-start | bytes 393224 | tf_op jit(solution)/shard_map/cond/branch_0_fun/ppermute | solution.py:38
  77.4 16.6 %copy-start.24 = (bf16[128,512]{1,0:T(8,128)(2,1)}, bf16[128,512]{1,0:T(8,128)(2,1)S(1)}, u32[]{:S(2)}) copy-start(bf16[128,512]{1,0:T(8,128)(2,1)S(1)} %collective-permute-done.2.beside_ref) | copy-start | bytes 393220 | tf_op jit(solution)/shard_map/cond
  77.4 16.5 %collective-permute-start.3 = (bf16[2,128,512]{2,1,0:T(8,128)(2,1)S(1)}, bf16[2,128,512]{2,1,0:T(8,128)(2,1)S(1)}, u32[]{:S(2)}, u32[]{:S(2)}) collective-permute-start(bf16[2,128,512]{2,1,0:T(8,128)(2,1)S(1)} %pad_maximum_fusion.4), channel_id=1, source_target_pairs={{0,2},{2,0},{1,3},{3,1},{4,6},{6,4},{5,7},{7,5},{8,10},{10,8},{9,1... | collective-permute-start | bytes 786440 | tf_op jit(solution)/shard_map/cond/branch_0_fun/ppermute | solution.py:38
  79.9 1.0 copy-start.12
  84.9 75.6 %all-to-all-start.2 = ((bf16[8,128,512]{2,1,0:T(8,128)(2,1)}), bf16[8,128,512]{2,1,0:T(8,128)(2,1)}, u32[]{:S(2)}, u32[]{:S(2)}) async-start(bf16[8,128,512]{2,1,0:T(8,128)(2,1)} %forward.3), calls=%async_computation.2 | async-start | bytes 2097152 | tf_op jit(solution)/shard_map/cond/branch_0_fun/all_to_all | solution.py:273
  94.0 5.9 %copy-start.30 = (bf16[2,128,512]{2,1,0:T(8,128)(2,1)}, bf16[2,128,512]{2,1,0:T(8,128)(2,1)S(1)}, u32[]{:S(2)}) copy-start(bf16[2,128,512]{2,1,0:T(8,128)(2,1)S(1)} %collective-permute-done.3.two_ref) | copy-start | bytes 786436 | tf_op jit(solution)/shard_map/cond
  94.0 5.9 %collective-permute-start.4 = (bf16[4,128,512]{2,1,0:T(8,128)(2,1)S(1)}, bf16[4,128,512]{2,1,0:T(8,128)(2,1)}, u32[]{:S(2)}, u32[]{:S(2)}) collective-permute-start(bf16[4,128,512]{2,1,0:T(8,128)(2,1)S(1)} %pad_maximum_fusion.1), channel_id=1, source_target_pairs={{0,1},{1,0},{2,3},{3,2},{4,5},{5,4},{6,7},{7,6},{8,9},{9,8},{10,11... | collective-permute-start | bytes 1572872 | tf_op jit(solution)/shard_map/cond/branch_0_fun/ppermute | solution.py:38
  103.4 35.4 %copy-start.15 = (f32[1,256,512]{2,1,0:T(8,128)S(1)}, f32[1,256,512]{2,1,0:T(8,128)}, u32[]{:S(2)}) copy-start(f32[1,256,512]{2,1,0:T(8,128)} %get-tuple-element.48) | copy-start | bytes 1572868 | tf_op jit(solution)/shard_map/cond
  103.4 35.4 %copy-start.18 = (f32[1,256,512]{2,1,0:T(8,128)S(1)}, f32[1,256,512]{2,1,0:T(8,128)}, u32[]{:S(2)}) copy-start(f32[1,256,512]{2,1,0:T(8,128)} %get-tuple-element.49) | copy-start | bytes 1572868 | tf_op jit(solution)/shard_map/cond
  106.5 18.9 %collective-permute-start.5 = (bf16[512,256]{1,0:T(8,128)(2,1)}, bf16[512,256]{1,0:T(8,128)(2,1)S(1)}, u32[]{:S(2)}, u32[]{:S(2)}) collective-permute-start(bf16[512,256]{1,0:T(8,128)(2,1)} %get-tuple-element.52), channel_id=1, source_target_pairs={{0,16},{8,24},{16,0},{24,8},{1,17},{9,25},{17,1},{25,9},{2,18},{10... | collective-permute-start | bytes 786440 | tf_op jit(solution)/shard_map/cond/branch_0_fun/ppermute | solution.py:25
  116.1 22.0 %collective-permute-start.6 = (bf16[512,256]{1,0:T(8,128)(2,1)}, bf16[512,256]{1,0:T(8,128)(2,1)S(1)}, u32[]{:S(2)}, u32[]{:S(2)}) collective-permute-start(bf16[512,256]{1,0:T(8,128)(2,1)} %get-tuple-element.53), channel_id=1, source_target_pairs={{0,8},{8,16},{16,24},{24,0},{1,9},{9,17},{17,25},{25,1},{2,10},{10... | collective-permute-start | bytes 786440 | tf_op jit(solution)/shard_map/cond/branch_0_fun/ppermute | solution.py:25
  119.4 18.6 %collective-permute-start.7 = (bf16[512,256]{1,0:T(8,128)(2,1)}, bf16[512,256]{1,0:T(8,128)(2,1)}, u32[]{:S(2)}, u32[]{:S(2)}) collective-permute-start(bf16[512,256]{1,0:T(8,128)(2,1)} %get-tuple-element.54), channel_id=1, source_target_pairs={{0,24},{8,0},{16,8},{24,16},{1,25},{9,1},{17,9},{25,17},{2,26},{10... | collective-permute-start | bytes 786440 | tf_op jit(solution)/shard_map/cond/branch_0_fun/ppermute | solution.py:25
  125.4 12.6 %copy-start.33 = (bf16[512,256]{1,0:T(8,128)(2,1)}, bf16[512,256]{1,0:T(8,128)(2,1)S(1)}, u32[]{:S(2)}) copy-start(bf16[512,256]{1,0:T(8,128)(2,1)S(1)} %collective-permute-done.5.refs_1_) | copy-start | bytes 786436 | tf_op jit(solution)/shard_map/cond
  138.0 0.7 copy-start.36
  141.3 17.4 %collective-permute-start.8 = (bf16[256,512]{1,0:T(8,128)(2,1)}, bf16[256,512]{1,0:T(8,128)(2,1)S(1)}, u32[]{:S(2)}, u32[]{:S(2)}) collective-permute-start(bf16[256,512]{1,0:T(8,128)(2,1)} %get-tuple-element.55), channel_id=1, source_target_pairs={{480,0},{0,32},{32,64},{64,96},{96,128},{128,160},{160,192},{192,2... | collective-permute-start | bytes 786440 | tf_op jit(solution)/shard_map/cond/branch_0_fun/ppermute | solution.py:281
